TPU v7x, 256 devices: a whole 4x4x8 slice. The times are simulated.
256 devices in a mesh: section: 4 (over x), blk: 64 (over y, z, core).
Axes of the slice: x: 4, y: 4, z: 8, core: 2. Of those that a mesh axis runs over, the one named last changes fastest.
Arguments:
- inputs: bfloat16 [4096, 8192], P(None, 'blk'), may hold values from -6 to 6
- cotangent: bfloat16 [4096, 8192], P(None, 'blk'), may hold values from -6 to 6
- r_weight: bfloat16 [4, 64, 128, 128], P('section', 'blk'), may hold values from -0.5 to 0.5
- g_weight: bfloat16 [4, 64, 128, 128], P('section', 'blk'), may hold values from -0.5 to 0.5
- l_weight: bfloat16 [4, 128, 64, 64], P('section', 'blk'), may hold values from -0.75 to 0.75
Outputs:
- input_grad: bfloat16 [4, 4096, 8192], P('section', None, 'blk')
- r_grad: float32 [4, 64, 128, 128], P('section', 'blk')
- g_grad: float32 [4, 64, 128, 128], P('section', 'blk')
- l_grad: float32 [4, 128, 64, 64], P('section', 'blk')
All inputs are finite; a program needn't handle non-finite values.
Results may differ from a plain program's by a relative error of at most 0.014.
Values may be sent and summed in bfloat16 or wider, within the bound.
No kernel may reach another device: no remote copies, remote signals or barrier semaphores. Data moves between devices by JAX's collectives and lax.ppermute only.
A program may use at most 192 MiB of HBM per device.

v0:
```python
import jax
import jax.numpy as jnp
from jax import lax
from jax.sharding import PartitionSpec as P

MICRO = 8


def passed_along(block, axis, distance):
    devices = range(lax.axis_size(axis))
    route = [(i - distance, i) for i in devices if i - distance in devices]
    return lax.ppermute(block, axis, route)


def layer_forward(rows_in, weights):
    r_w, g_w, l_w = weights
    count = rows_in.shape[0]
    blocks = rows_in.reshape(count, r_w.shape[0], r_w.shape[1])
    first = jnp.einsum("nbj,bjk->nbk", blocks, r_w, preferred_element_type=jnp.float32).astype(
        jnp.bfloat16
    )
    permuted = lax.all_to_all(first, "blk", split_axis=2, concat_axis=1, tiled=True)
    mixed = jnp.einsum("nbk,kbc->nck", permuted, l_w, preferred_element_type=jnp.float32).astype(
        jnp.bfloat16
    )
    mixed = lax.all_to_all(mixed, "blk", split_axis=1, concat_axis=2, tiled=True)
    mixed, permuted = (mixed, permuted)
    gate = jnp.einsum("nbj,bjk->nbk", blocks, g_w, preferred_element_type=jnp.float32)
    result = blocks.astype(jnp.float32) + mixed.astype(jnp.float32) * jax.nn.sigmoid(gate)
    return (result.astype(jnp.bfloat16).reshape(count, -1), (blocks, permuted, mixed, gate))


def layer_backward(grad_rows, saved, weights):
    r_w, g_w, l_w = weights
    blocks, permuted, mixed, gate = saved
    count = blocks.shape[0]
    upper = grad_rows.reshape(blocks.shape).astype(jnp.float32)
    sig = jax.nn.sigmoid(gate)
    grad_mixed = (upper * sig).astype(jnp.bfloat16)
    grad_gate = (upper * mixed.astype(jnp.float32) * sig * (1.0 - sig)).astype(jnp.bfloat16)
    mixed_cols = lax.all_to_all(grad_mixed, "blk", split_axis=2, concat_axis=1, tiled=True)
    grad_first = jnp.einsum(
        "nck,kbc->nbk", mixed_cols, l_w, preferred_element_type=jnp.float32
    ).astype(jnp.bfloat16)
    l_part = jnp.einsum("nbk,nck->kbc", permuted, mixed_cols, preferred_element_type=jnp.float32)
    first_rows = lax.all_to_all(grad_first, "blk", split_axis=1, concat_axis=2, tiled=True)
    lower = upper + jnp.einsum("nbk,bjk->nbj", first_rows, r_w, preferred_element_type=jnp.float32)
    lower = lower + jnp.einsum("nbk,bjk->nbj", grad_gate, g_w, preferred_element_type=jnp.float32)
    r_part = jnp.einsum("nbj,nbk->bjk", blocks, first_rows, preferred_element_type=jnp.float32)
    g_part = jnp.einsum("nbj,nbk->bjk", blocks, grad_gate, preferred_element_type=jnp.float32)
    return (lower.astype(jnp.bfloat16).reshape(count, -1), (r_part, g_part, l_part))


def keep_slot(buffer, value, place, valid):
    older = lax.dynamic_index_in_dim(buffer, place, 0, keepdims=False)
    return lax.dynamic_update_index_in_dim(buffer, jnp.where(valid, value, older), place, 0)


def run_sections(inputs, cotangent, weights, micro):
    sections = lax.axis_size("section")
    member = lax.axis_index("section")
    rows = inputs.shape[0] // micro
    carry = None
    buffers = None
    for step_idx in range(micro + sections - 1):
        fresh = lax.dynamic_slice_in_dim(inputs, min(step_idx, micro - 1) * rows, rows, 0)
        if step_idx > 0:
            arrived = passed_along(carry, "section", 1)
            rows_in = jnp.where(member == 0, fresh, arrived)
        else:
            rows_in = fresh
        result, saved = layer_forward(rows_in, weights)
        slot = step_idx - member
        valid = (slot >= 0) & (slot < micro)
        place = jnp.clip(slot, 0, micro - 1)
        if buffers is None:
            buffers = tuple((jnp.zeros((micro,) + piece.shape, piece.dtype) for piece in saved))
        buffers = tuple((keep_slot(buf, piece, place, valid) for buf, piece in zip(buffers, saved)))
        carry = result
    grads_out = jnp.zeros_like(inputs)
    totals = None
    carry = None
    for step_idx in range(micro + sections - 1):
        fresh = lax.dynamic_slice_in_dim(cotangent, min(step_idx, micro - 1) * rows, rows, 0)
        if step_idx > 0:
            arrived = passed_along(carry, "section", -1)
            grad_in = jnp.where(member == sections - 1, fresh, arrived)
        else:
            grad_in = fresh
        slot = step_idx - (sections - 1 - member)
        valid = (slot >= 0) & (slot < micro)
        place = jnp.clip(slot, 0, micro - 1)
        saved = tuple((lax.dynamic_index_in_dim(buf, place, 0, keepdims=False) for buf in buffers))
        lower, parts = layer_backward(grad_in, saved, weights)
        parts = tuple((jnp.where(valid, piece, 0.0) for piece in parts))
        if totals is None:
            totals = parts
        else:
            totals = tuple((acc + piece for acc, piece in zip(totals, parts)))
        older = lax.dynamic_slice_in_dim(grads_out, place * rows, rows, 0)
        grads_out = lax.dynamic_update_slice_in_dim(
            grads_out, jnp.where(valid, lower, older), place * rows, 0
        )
        carry = lower
    return (grads_out, totals)


def shards(inputs, cotangent, r_weight, g_weight, l_weight):
    weights = (r_weight[0], g_weight[0], l_weight[0])
    grads_out, totals = run_sections(inputs, cotangent, weights, MICRO)
    r_total, g_total, l_total = totals
    return (grads_out[None], r_total[None], g_total[None], l_total[None])


def solution(mesh):
    return jax.shard_map(
        shards,
        mesh=mesh,
        in_specs=(
            P(None, "blk"),
            P(None, "blk"),
            P("section", "blk", None, None),
            P("section", "blk", None, None),
            P("section", "blk", None, None),
        ),
        out_specs=(
            P("section", None, "blk"),
            P("section", "blk", None, None),
            P("section", "blk", None, None),
            P("section", "blk", None, None),
        ),
        check_vma=False,
    )
```

profile of v0, /device:TPU:1, one launch (start us, length us, event | category | flops | bytes accessed | tf_op | source)
XLA Modules:
  0.0 1221.2 jit_solution(14283230373066580237)
XLA Ops:
  4.8 13.1 %all-to-all-start = ((bf16[64,2,512]{2,1,0:T(2,128)(2,1)}), bf16[64,2,512]{2,1,0:T(2,128)(2,1)S(1)}, u32[]{:S(2)}, u32[]{:S(2)}) async-start(bf16[64,2,512]{2,1,0:T(2,128)(2,1)} %reshape.1322), calls=%async_computation | async-start | bytes 262144 | tf_op jit(solution)/shard_map/all_to_all | solution.py:22
  18.0 10.3 all-to-all-done
  38.3 8.1 all-to-all-done.1
  60.6 16.0 %all_to_all.522 = bf16[64,2,512]{2,1,0:T(2,128)(2,1)S(1)} all-to-all(bf16[64,2,512]{2,1,0:T(2,128)(2,1)} %reshape.1324), channel_id=1, replica_groups=mesh['section'=4,'blk'=64] {'blk'}, dimensions={0} | all-to-all | bytes 262144 | tf_op jit(solution)/shard_map/all_to_all | solution.py:22
  87.9 9.4 all-to-all-done.3
  112.6 16.0 %all_to_all.523 = bf16[64,2,512]{2,1,0:T(2,128)(2,1)S(1)} all-to-all(bf16[64,2,512]{2,1,0:T(2,128)(2,1)} %reshape.1326), channel_id=1, replica_groups=mesh['section'=4,'blk'=64] {'blk'}, dimensions={0} | all-to-all | bytes 262144 | tf_op jit(solution)/shard_map/all_to_all | solution.py:22
  139.9 9.4 all-to-all-done.5
  164.7 16.0 %all_to_all.524 = bf16[64,2,512]{2,1,0:T(2,128)(2,1)S(1)} all-to-all(bf16[64,2,512]{2,1,0:T(2,128)(2,1)} %reshape.1328), channel_id=1, replica_groups=mesh['section'=4,'blk'=64] {'blk'}, dimensions={0} | all-to-all | bytes 262144 | tf_op jit(solution)/shard_map/all_to_all | solution.py:22
  185.8 5.2 all-to-all-start.7
  192.0 9.4 all-to-all-done.7
  216.8 16.0 %all_to_all.525 = bf16[64,2,512]{2,1,0:T(2,128)(2,1)S(1)} all-to-all(bf16[64,2,512]{2,1,0:T(2,128)(2,1)} %reshape.1330), channel_id=1, replica_groups=mesh['section'=4,'blk'=64] {'blk'}, dimensions={0} | all-to-all | bytes 262144 | tf_op jit(solution)/shard_map/all_to_all | solution.py:22
  237.9 5.4 all-to-all-start.9
  244.3 9.4 all-to-all-done.9
  269.1 16.0 %all_to_all.526 = bf16[64,2,512]{2,1,0:T(2,128)(2,1)S(1)} all-to-all(bf16[64,2,512]{2,1,0:T(2,128)(2,1)} %reshape.1332), channel_id=1, replica_groups=mesh['section'=4,'blk'=64] {'blk'}, dimensions={0} | all-to-all | bytes 262144 | tf_op jit(solution)/shard_map/all_to_all | solution.py:22
  296.3 9.4 all-to-all-done.11
  320.2 16.0 %all_to_all.527 = bf16[64,2,512]{2,1,0:T(2,128)(2,1)S(1)} all-to-all(bf16[64,2,512]{2,1,0:T(2,128)(2,1)} %reshape.1334), channel_id=1, replica_groups=mesh['section'=4,'blk'=64] {'blk'}, dimensions={0} | all-to-all | bytes 262144 | tf_op jit(solution)/shard_map/all_to_all | solution.py:22
  347.5 9.4 all-to-all-done.13
  360.3 5.7 collective-permute-start.6
  378.3 5.9 all-to-all-start.14
  402.4 7.8 all-to-all-start.15
  411.2 9.3 all-to-all-done.15
  437.6 5.5 all-to-all-start.16
  461.3 6.8 all-to-all-start.17
  469.1 9.3 all-to-all-done.17
  497.4 5.8 all-to-all-start.18
  521.3 7.0 all-to-all-start.19
  529.2 9.3 all-to-all-done.19
  565.1 6.4 all-to-all-done.22
  584.6 7.5 all-to-all-done.23
  602.6 15.2 %all_to_all.528 = bf16[64,2,512]{2,1,0:T(2,128)(2,1)S(1)} all-to-all(bf16[64,2,512]{2,1,0:T(2,128)(2,1)} %reshape.1344), channel_id=1, replica_groups=mesh['section'=4,'blk'=64] {'blk'}, dimensions={0} | all-to-all | bytes 262144 | tf_op jit(solution)/shard_map/all_to_all | solution.py:41
  622.9 5.4 all-to-all-start.21
  630.1 8.6 all-to-all-done.21
  657.6 15.7 %all_to_all.529 = bf16[64,2,512]{2,1,0:T(2,128)(2,1)S(1)} all-to-all(bf16[64,2,512]{2,1,0:T(2,128)(2,1)} %reshape.1346), channel_id=1, replica_groups=mesh['section'=4,'blk'=64] {'blk'}, dimensions={0} | all-to-all | bytes 262144 | tf_op jit(solution)/shard_map/all_to_all | solution.py:41
  678.4 5.2 all-to-all-start.25
  683.6 10.4 all-to-all-done.25
  711.8 6.1 all-to-all-start.26
  738.9 11.2 all-to-all-start.27
  779.7 7.2 all-to-all-start.28
  804.9 6.1 all-to-all-start.29
  840.8 7.0 all-to-all-start.30
  851.9 6.2 all-to-all-done.30
  865.9 5.4 all-to-all-start.31
  875.4 6.2 all-to-all-done.31
  899.0 6.1 all-to-all-start.32
  907.7 7.8 all-to-all-done.32
  931.1 7.8 all-to-all-done.33
  957.1 6.1 all-to-all-start.34
  965.7 7.8 all-to-all-done.34
  981.3 5.4 all-to-all-start.35
  989.6 7.5 all-to-all-done.35
  1014.5 6.1 all-to-all-start.36
  1024.2 6.8 all-to-all-done.36
  1047.4 6.9 all-to-all-done.37
  1072.5 6.1 all-to-all-start.38
  1081.1 7.8 all-to-all-done.38
  1096.7 5.6 all-to-all-start.39
  1104.9 7.6 all-to-all-done.39
  1130.0 6.0 all-to-all-start.40
  1139.8 6.6 all-to-all-done.40
  1154.2 5.2 all-to-all-start.41
  1162.1 7.7 all-to-all-done.41
  1184.1 5.6 all-to-all-start.42
  1192.7 7.4 all-to-all-done.42
  1209.6 7.5 all-to-all-done.43
  (565 shorter events, 680.7 us)
Async XLA Ops:
  0.6 36.7 %copy-start = (bf16[1,1,128,128]{3,2,1,0:T(8,128)(2,1)S(1)}, bf16[1,1,128,128]{3,2,1,0:T(8,128)(2,1)}, u32[]{:S(2)}) copy-start(bf16[1,1,128,128]{3,2,1,0:T(8,128)(2,1)} %param.8) | copy-start | bytes 98308
  0.6 35.4 %copy-start.4 = (bf16[4096,128]{1,0:T(8,128)(2,1)S(1)}, bf16[4096,128]{1,0:T(8,128)(2,1)}, u32[]{:S(2)}) copy-start(bf16[4096,128]{1,0:T(8,128)(2,1)} %param.5) | copy-start | bytes 3145732
  0.7 29.4 %copy-start.1 = (bf16[1,2,64,64]{3,2,1,0:T(8,128)(2,1)S(1)}, bf16[1,2,64,64]{3,2,1,0:T(8,128)(2,1)}, u32[]{:S(2)}) copy-start(bf16[1,2,64,64]{3,2,1,0:T(8,128)(2,1)} %param.9) | copy-start | bytes 49156
  4.8 23.5 %all-to-all-start = ((bf16[64,2,512]{2,1,0:T(2,128)(2,1)}), bf16[64,2,512]{2,1,0:T(2,128)(2,1)S(1)}, u32[]{:S(2)}, u32[]{:S(2)}) async-start(bf16[64,2,512]{2,1,0:T(2,128)(2,1)} %reshape.1322), calls=%async_computation | async-start | bytes 262144 | tf_op jit(solution)/shard_map/all_to_all | solution.py:22
  31.1 15.2 %all-to-all-start.1 = ((bf16[512,64,2]{0,2,1:T(2,128)(2,1)}), bf16[512,64,2]{0,2,1:T(2,128)(2,1)S(1)}, u32[]{:S(2)}, u32[]{:S(2)}) async-start(bf16[512,64,2]{0,2,1:T(2,128)(2,1)} %copy.422), calls=%async_computation.1 | async-start | bytes 262144 | tf_op jit(solution)/shard_map/all_to_all | solution.py:26
  48.1 5.9 collective-permute-start
  81.7 15.5 %all-to-all-start.3 = ((bf16[512,64,2]{0,2,1:T(2,128)(2,1)}), bf16[512,64,2]{0,2,1:T(2,128)(2,1)}, u32[]{:S(2)}, u32[]{:S(2)}) async-start(bf16[512,64,2]{0,2,1:T(2,128)(2,1)} %copy.428), calls=%async_computation.3 | async-start | bytes 262144 | tf_op jit(solution)/shard_map/all_to_all | solution.py:26
  100.6 6.9 collective-permute-start.1
  133.8 15.5 %all-to-all-start.5 = ((bf16[512,64,2]{0,2,1:T(2,128)(2,1)}), bf16[512,64,2]{0,2,1:T(2,128)(2,1)}, u32[]{:S(2)}, u32[]{:S(2)}) async-start(bf16[512,64,2]{0,2,1:T(2,128)(2,1)} %copy.434), calls=%async_computation.5 | async-start | bytes 262144 | tf_op jit(solution)/shard_map/all_to_all | solution.py:26
  152.7 6.9 collective-permute-start.2
  185.8 15.6 %all-to-all-start.7 = ((bf16[512,64,2]{0,2,1:T(2,128)(2,1)}), bf16[512,64,2]{0,2,1:T(2,128)(2,1)}, u32[]{:S(2)}, u32[]{:S(2)}) async-start(bf16[512,64,2]{0,2,1:T(2,128)(2,1)} %copy.440), calls=%async_computation.7 | async-start | bytes 262144 | tf_op jit(solution)/shard_map/all_to_all | solution.py:26
  204.8 6.9 collective-permute-start.3
  235.2 28.3 %copy-start.10 = (bf16[512,128]{0,1:T(8,128)(2,1)}, bf16[512,128]{0,1:T(8,128)(2,1)S(1)}, u32[]{:S(2)}) copy-start(bf16[512,128]{0,1:T(8,128)(2,1)S(1)} %bitcast_reduce_fusion.17) | copy-start | bytes 393220
  237.9 15.8 %all-to-all-start.9 = ((bf16[512,64,2]{0,2,1:T(2,128)(2,1)}), bf16[512,64,2]{0,2,1:T(2,128)(2,1)}, u32[]{:S(2)}, u32[]{:S(2)}) async-start(bf16[512,64,2]{0,2,1:T(2,128)(2,1)} %copy.446), calls=%async_computation.9 | async-start | bytes 262144 | tf_op jit(solution)/shard_map/all_to_all | solution.py:26
  257.1 6.9 collective-permute-start.4
  290.2 15.5 %all-to-all-start.11 = ((bf16[512,64,2]{0,2,1:T(2,128)(2,1)}), bf16[512,64,2]{0,2,1:T(2,128)(2,1)}, u32[]{:S(2)}, u32[]{:S(2)}) async-start(bf16[512,64,2]{0,2,1:T(2,128)(2,1)} %copy.452), calls=%async_computation.11 | async-start | bytes 262144 | tf_op jit(solution)/shard_map/all_to_all | solution.py:26
  309.1 6.9 collective-permute-start.5
  338.7 29.5 %copy-start.14 = (bf16[512,128]{0,1:T(8,128)(2,1)}, bf16[512,128]{0,1:T(8,128)(2,1)S(1)}, u32[]{:S(2)}) copy-start(bf16[512,128]{0,1:T(8,128)(2,1)S(1)} %bitcast_reduce_fusion.15) | copy-start | bytes 393220
  341.3 15.6 %all-to-all-start.13 = ((bf16[512,64,2]{0,2,1:T(2,128)(2,1)}), bf16[512,64,2]{0,2,1:T(2,128)(2,1)}, u32[]{:S(2)}, u32[]{:S(2)}) async-start(bf16[512,64,2]{0,2,1:T(2,128)(2,1)} %copy.458), calls=%async_computation.13 | async-start | bytes 262144 | tf_op jit(solution)/shard_map/all_to_all | solution.py:26
  360.3 10.7 collective-permute-start.6
  378.3 16.3 %all-to-all-start.14 = ((bf16[64,2,512]{2,1,0:T(2,128)(2,1)}), bf16[64,2,512]{2,1,0:T(2,128)(2,1)}, u32[]{:S(2)}, u32[]{:S(2)}) async-start(bf16[64,2,512]{2,1,0:T(2,128)(2,1)} %reshape.1336), calls=%async_computation.14 | async-start | bytes 262144 | tf_op jit(solution)/shard_map/all_to_all | solution.py:22
  402.4 18.1 %all-to-all-start.15 = ((bf16[512,64,2]{0,2,1:T(2,128)(2,1)}), bf16[512,64,2]{0,2,1:T(2,128)(2,1)}, u32[]{:S(2)}, u32[]{:S(2)}) async-start(bf16[512,64,2]{0,2,1:T(2,128)(2,1)} %copy.463), calls=%async_computation.15 | async-start | bytes 262144 | tf_op jit(solution)/shard_map/all_to_all | solution.py:26
  423.9 6.4 collective-permute-start.7
  437.6 15.9 %all-to-all-start.16 = ((bf16[64,2,512]{2,1,0:T(2,128)(2,1)}), bf16[64,2,512]{2,1,0:T(2,128)(2,1)}, u32[]{:S(2)}, u32[]{:S(2)}) async-start(bf16[64,2,512]{2,1,0:T(2,128)(2,1)} %reshape.1338), calls=%async_computation.16 | async-start | bytes 262144 | tf_op jit(solution)/shard_map/all_to_all | solution.py:22
  461.3 17.1 %all-to-all-start.17 = ((bf16[512,64,2]{0,2,1:T(2,128)(2,1)}), bf16[512,64,2]{0,2,1:T(2,128)(2,1)}, u32[]{:S(2)}, u32[]{:S(2)}) async-start(bf16[512,64,2]{0,2,1:T(2,128)(2,1)} %copy.468), calls=%async_computation.17 | async-start | bytes 262144 | tf_op jit(solution)/shard_map/all_to_all | solution.py:26
  481.8 8.3 collective-permute-start.8
  497.4 16.0 %all-to-all-start.18 = ((bf16[64,2,512]{2,1,0:T(2,128)(2,1)}), bf16[64,2,512]{2,1,0:T(2,128)(2,1)}, u32[]{:S(2)}, u32[]{:S(2)}) async-start(bf16[64,2,512]{2,1,0:T(2,128)(2,1)} %reshape.1340), calls=%async_computation.18 | async-start | bytes 262144 | tf_op jit(solution)/shard_map/all_to_all | solution.py:22
  521.3 17.2 %all-to-all-start.19 = ((bf16[512,64,2]{0,2,1:T(2,128)(2,1)}), bf16[512,64,2]{0,2,1:T(2,128)(2,1)}, u32[]{:S(2)}, u32[]{:S(2)}) async-start(bf16[512,64,2]{0,2,1:T(2,128)(2,1)} %copy.473), calls=%async_computation.19 | async-start | bytes 262144 | tf_op jit(solution)/shard_map/all_to_all | solution.py:26
  541.9 7.7 collective-permute-start.9
  556.0 15.5 %all-to-all-start.22 = ((bf16[64,2,512]{2,1,0:T(2,128)(2,1)}), bf16[64,2,512]{2,1,0:T(2,128)(2,1)S(1)}, u32[]{:S(2)}, u32[]{:S(2)}) async-start(bf16[64,2,512]{2,1,0:T(2,128)(2,1)} %reshape.1342), calls=%async_computation.22 | async-start | bytes 262144 | tf_op jit(solution)/shard_map/all_to_all | solution.py:22
  562.7 32.6 %copy-start.26 = (bf16[512,128]{0,1:T(8,128)(2,1)S(1)}, bf16[512,128]{0,1:T(8,128)(2,1)}, u32[]{:S(2)}) copy-start(bf16[512,128]{0,1:T(8,128)(2,1)} %copy.640) | copy-start | bytes 393220
  576.6 15.5 %all-to-all-start.23 = ((bf16[512,64,2]{0,2,1:T(2,128)(2,1)}), bf16[512,64,2]{0,2,1:T(2,128)(2,1)}, u32[]{:S(2)}, u32[]{:S(2)}) async-start(bf16[512,64,2]{0,2,1:T(2,128)(2,1)} %copy.482), calls=%async_computation.23 | async-start | bytes 262144 | tf_op jit(solution)/shard_map/all_to_all | solution.py:26
  622.9 15.8 %all-to-all-start.21 = ((bf16[512,64,2]{0,2,1:T(2,128)(2,1)}), bf16[512,64,2]{0,2,1:T(2,128)(2,1)}, u32[]{:S(2)}, u32[]{:S(2)}) async-start(bf16[512,64,2]{0,2,1:T(2,128)(2,1)} %copy.477), calls=%async_computation.21 | async-start | bytes 262144 | tf_op jit(solution)/shard_map/all_to_all | solution.py:46
  642.5 7.7 collective-permute-start.10
  678.4 15.6 %all-to-all-start.25 = ((bf16[512,64,2]{0,2,1:T(2,128)(2,1)}), bf16[512,64,2]{0,2,1:T(2,128)(2,1)}, u32[]{:S(2)}, u32[]{:S(2)}) async-start(bf16[512,64,2]{0,2,1:T(2,128)(2,1)} %copy.487), calls=%async_computation.25 | async-start | bytes 262144 | tf_op jit(solution)/shard_map/all_to_all | solution.py:46
  697.0 6.9 collective-permute-start.11
  711.8 19.3 %all-to-all-start.26 = ((bf16[64,2,512]{2,1,0:T(2,128)(2,1)}), bf16[64,2,512]{2,1,0:T(2,128)(2,1)}, u32[]{:S(2)}, u32[]{:S(2)}) async-start(bf16[64,2,512]{2,1,0:T(2,128)(2,1)} %reshape.1348), calls=%async_computation.26 | async-start | bytes 262144 | tf_op jit(solution)/shard_map/all_to_all | solution.py:41
  738.9 21.3 %all-to-all-start.27 = ((bf16[512,64,2]{0,2,1:T(2,128)(2,1)}), bf16[512,64,2]{0,2,1:T(2,128)(2,1)}, u32[]{:S(2)}, u32[]{:S(2)}) async-start(bf16[512,64,2]{0,2,1:T(2,128)(2,1)} %copy.493), calls=%async_computation.27 | async-start | bytes 262144 | tf_op jit(solution)/shard_map/all_to_all | solution.py:46
  764.8 6.9 collective-permute-start.12
  779.7 17.5 %all-to-all-start.28 = ((bf16[64,2,512]{2,1,0:T(2,128)(2,1)}), bf16[64,2,512]{2,1,0:T(2,128)(2,1)}, u32[]{:S(2)}, u32[]{:S(2)}) async-start(bf16[64,2,512]{2,1,0:T(2,128)(2,1)} %reshape.1350), calls=%async_computation.28 | async-start | bytes 262144 | tf_op jit(solution)/shard_map/all_to_all | solution.py:41
  804.9 16.4 %all-to-all-start.29 = ((bf16[512,64,2]{0,2,1:T(2,128)(2,1)}), bf16[512,64,2]{0,2,1:T(2,128)(2,1)}, u32[]{:S(2)}, u32[]{:S(2)}) async-start(bf16[512,64,2]{0,2,1:T(2,128)(2,1)} %copy.499), calls=%async_computation.29 | async-start | bytes 262144 | tf_op jit(solution)/shard_map/all_to_all | solution.py:46
  825.9 6.9 collective-permute-start.13
  840.8 17.2 %all-to-all-start.30 = ((bf16[64,2,512]{2,1,0:T(2,128)(2,1)}), bf16[64,2,512]{2,1,0:T(2,128)(2,1)}, u32[]{:S(2)}, u32[]{:S(2)}) async-start(bf16[64,2,512]{2,1,0:T(2,128)(2,1)} %reshape.1352), calls=%async_computation.30 | async-start | bytes 262144 | tf_op jit(solution)/shard_map/all_to_all | solution.py:41
  865.9 15.8 %all-to-all-start.31 = ((bf16[512,64,2]{0,2,1:T(2,128)(2,1)}), bf16[512,64,2]{0,2,1:T(2,128)(2,1)}, u32[]{:S(2)}, u32[]{:S(2)}) async-start(bf16[512,64,2]{0,2,1:T(2,128)(2,1)} %copy.505), calls=%async_computation.31 | async-start | bytes 262144 | tf_op jit(solution)/shard_map/all_to_all | solution.py:46
  875.4 29.7 %copy-start.25 = (bf16[512,128]{0,1:T(8,128)(2,1)S(1)}, bf16[512,128]{0,1:T(8,128)(2,1)}, u32[]{:S(2)}) copy-start(bf16[512,128]{0,1:T(8,128)(2,1)} %copy-done.24) | copy-start | bytes 393220
  886.2 6.5 collective-permute-start.14
  899.0 16.4 %all-to-all-start.32 = ((bf16[64,2,512]{2,1,0:T(2,128)(2,1)}), bf16[64,2,512]{2,1,0:T(2,128)(2,1)}, u32[]{:S(2)}, u32[]{:S(2)}) async-start(bf16[64,2,512]{2,1,0:T(2,128)(2,1)} %reshape.1354), calls=%async_computation.32 | async-start | bytes 262144 | tf_op jit(solution)/shard_map/all_to_all | solution.py:41
  923.3 15.6 %all-to-all-start.33 = ((bf16[512,64,2]{0,2,1:T(2,128)(2,1)}), bf16[512,64,2]{0,2,1:T(2,128)(2,1)}, u32[]{:S(2)}, u32[]{:S(2)}) async-start(bf16[512,64,2]{0,2,1:T(2,128)(2,1)} %copy.511), calls=%async_computation.33 | async-start | bytes 262144 | tf_op jit(solution)/shard_map/all_to_all | solution.py:46
  942.5 6.7 collective-permute-start.15
  957.1 16.4 %all-to-all-start.34 = ((bf16[64,2,512]{2,1,0:T(2,128)(2,1)}), bf16[64,2,512]{2,1,0:T(2,128)(2,1)}, u32[]{:S(2)}, u32[]{:S(2)}) async-start(bf16[64,2,512]{2,1,0:T(2,128)(2,1)} %reshape.1356), calls=%async_computation.34 | async-start | bytes 262144 | tf_op jit(solution)/shard_map/all_to_all | solution.py:41
  981.3 15.8 %all-to-all-start.35 = ((bf16[512,64,2]{0,2,1:T(2,128)(2,1)}), bf16[512,64,2]{0,2,1:T(2,128)(2,1)}, u32[]{:S(2)}, u32[]{:S(2)}) async-start(bf16[512,64,2]{0,2,1:T(2,128)(2,1)} %copy.517), calls=%async_computation.35 | async-start | bytes 262144 | tf_op jit(solution)/shard_map/all_to_all | solution.py:46
  1000.1 6.5 collective-permute-start.16
  1009.0 35.0 %copy-start.23 = (bf16[512,128]{0,1:T(8,128)(2,1)S(1)}, bf16[512,128]{0,1:T(8,128)(2,1)}, u32[]{:S(2)}) copy-start(bf16[512,128]{0,1:T(8,128)(2,1)} %copy-done.22) | copy-start | bytes 393220
  1014.5 16.4 %all-to-all-start.36 = ((bf16[64,2,512]{2,1,0:T(2,128)(2,1)}), bf16[64,2,512]{2,1,0:T(2,128)(2,1)}, u32[]{:S(2)}, u32[]{:S(2)}) async-start(bf16[64,2,512]{2,1,0:T(2,128)(2,1)} %reshape.1358), calls=%async_computation.36 | async-start | bytes 262144 | tf_op jit(solution)/shard_map/all_to_all | solution.py:41
  1038.7 15.6 %all-to-all-start.37 = ((bf16[512,64,2]{0,2,1:T(2,128)(2,1)}), bf16[512,64,2]{0,2,1:T(2,128)(2,1)}, u32[]{:S(2)}, u32[]{:S(2)}) async-start(bf16[512,64,2]{0,2,1:T(2,128)(2,1)} %copy.523), calls=%async_computation.37 | async-start | bytes 262144 | tf_op jit(solution)/shard_map/all_to_all | solution.py:46
  1058.0 6.5 collective-permute-start.17
  1072.5 16.4 %all-to-all-start.38 = ((bf16[64,2,512]{2,1,0:T(2,128)(2,1)}), bf16[64,2,512]{2,1,0:T(2,128)(2,1)}, u32[]{:S(2)}, u32[]{:S(2)}) async-start(bf16[64,2,512]{2,1,0:T(2,128)(2,1)} %reshape.1360), calls=%async_computation.38 | async-start | bytes 262144 | tf_op jit(solution)/shard_map/all_to_all | solution.py:41
  1096.7 15.8 %all-to-all-start.39 = ((bf16[512,64,2]{0,2,1:T(2,128)(2,1)}), bf16[512,64,2]{0,2,1:T(2,128)(2,1)}, u32[]{:S(2)}, u32[]{:S(2)}) async-start(bf16[512,64,2]{0,2,1:T(2,128)(2,1)} %copy.528), calls=%async_computation.39 | async-start | bytes 262144 | tf_op jit(solution)/shard_map/all_to_all | solution.py:46
  1115.6 6.5 collective-permute-start.18
  1130.0 16.4 %all-to-all-start.40 = ((bf16[64,2,512]{2,1,0:T(2,128)(2,1)}), bf16[64,2,512]{2,1,0:T(2,128)(2,1)}, u32[]{:S(2)}, u32[]{:S(2)}) async-start(bf16[64,2,512]{2,1,0:T(2,128)(2,1)} %reshape.1362), calls=%async_computation.40 | async-start | bytes 262144 | tf_op jit(solution)/shard_map/all_to_all | solution.py:41
  1154.2 15.6 %all-to-all-start.41 = ((bf16[512,64,2]{0,2,1:T(2,128)(2,1)}), bf16[512,64,2]{0,2,1:T(2,128)(2,1)}, u32[]{:S(2)}, u32[]{:S(2)}) async-start(bf16[512,64,2]{0,2,1:T(2,128)(2,1)} %copy.533), calls=%async_computation.41 | async-start | bytes 262144 | tf_op jit(solution)/shard_map/all_to_all | solution.py:46
  1172.8 6.5 collective-permute-start.19
  1184.1 16.0 %all-to-all-start.42 = ((bf16[64,2,512]{2,1,0:T(2,128)(2,1)}), bf16[64,2,512]{2,1,0:T(2,128)(2,1)S(1)}, u32[]{:S(2)}, u32[]{:S(2)}) async-start(bf16[64,2,512]{2,1,0:T(2,128)(2,1)} %reshape.1364), calls=%async_computation.42 | async-start | bytes 262144 | tf_op jit(solution)/shard_map/all_to_all | solution.py:41
  1201.9 15.2 %all-to-all-start.43 = ((bf16[512,64,2]{0,2,1:T(2,128)(2,1)}), bf16[512,64,2]{0,2,1:T(2,128)(2,1)S(1)}, u32[]{:S(2)}, u32[]{:S(2)}) async-start(bf16[512,64,2]{0,2,1:T(2,128)(2,1)} %copy.538), calls=%async_computation.43 | async-start | bytes 262144 | tf_op jit(solution)/shard_map/all_to_all | solution.py:46
  (43 other events, 653.7 us)
where the time goes:
time: 1240 us; the launch traced here: 1220 us
  waiting for transfers between devices  298 us (24%)
  starting transfers between devices  278 us (22%)
  local copies, waits for them, and re-layouts  268 us (22%)
  other arithmetic  136 us (11%)
  blocking collectives  127 us (10%)
  matrix products  111 us (9%)
    all_to_all x11, waiting for transfers between devices, layer_forward(): lax.all_to_all(mixed, 'blk', split_axis=1, concat_axis=2, tiled=True)  99.8 us
    all_to_all x6, blocking collectives, layer_forward(): lax.all_to_all(first, 'blk', split_axis=2, concat_axis=1, tiled=True)  95.8 us
    unnamed x165, local copies, waits for them, and re-layouts  91.1 us
    all_to_all x11, waiting for transfers between devices, layer_backward(): lax.all_to_all(grad_first, 'blk', split_axis=1, concat_axis=2, tiled=True)  78.8 us
    all_to_all x11, starting transfers between devices, layer_backward(): lax.all_to_all(grad_first, 'blk', split_axis=1, concat_axis=2, tiled=True)  64.9 us
    all_to_all x11, starting transfers between devices, layer_forward(): lax.all_to_all(mixed, 'blk', split_axis=1, concat_axis=2, tiled=True)  62.9 us
    ppermute x20, starting transfers between devices, passed_along(): return lax.ppermute(block, axis, route)  58.6 us
    unnamed x22, other arithmetic  57.9 us
  transfers between devices with their start and end apart: 56, of which 51 were waited for; matrix products, arithmetic and copies ran while one was open for 11% of the time, Pallas kernels for 0%

commit v1 on v0

v1 whole, which is shorter than its diff:
```python
import functools

import jax
import jax.numpy as jnp
from jax import lax
from jax.experimental import pallas as pl
from jax.experimental.pallas import tpu as pltpu
from jax.sharding import Mesh, PartitionSpec as P

BF = jnp.bfloat16
F32 = jnp.float32
CHUNKS = 2


def nn(a, b):
    return lax.dot_general(a, b, (((1,), (0,)), ((), ())), preferred_element_type=F32)


def nt(a, b):
    return lax.dot_general(a, b, (((1,), (1,)), ((), ())), preferred_element_type=F32)


def feature_order(rows, cols, transposed=False):
    r = lax.broadcasted_iota(jnp.int32, (rows, cols), 1 if transposed else 0)
    c = lax.broadcasted_iota(jnp.int32, (rows, cols), 0 if transposed else 1)
    natural = ((r >> 2) & 1) * 128 + (r >> 3) * 4 + (r & 3)
    return jnp.where(natural == c, 1.0, 0.0).astype(BF)


def position_order(rows, cols, transposed=False):
    r = lax.broadcasted_iota(jnp.int32, (rows, cols), 1 if transposed else 0)
    c = lax.broadcasted_iota(jnp.int32, (rows, cols), 0 if transposed else 1)
    natural = (r & 3) * 64 + (r >> 3) * 2 + ((r >> 2) & 1)
    return jnp.where(natural == c, 1.0, 0.0).astype(BF)


def rows_of(ref):
    d, i, n = ref.shape
    return ref[...].astype(F32).reshape(d * i, n)


def put_rows(ref, value):
    ref[...] = value.reshape(ref.shape).astype(ref.dtype)


def prepare_kernel(w_ref, r_ref, rt_ref, g_ref, gt_ref, l_ref, lt_ref):
    p = feature_order(256, 256)
    q = position_order(256, 256)
    for start, plain, flipped in ((0, r_ref, rt_ref), (128, g_ref, gt_ref)):
        blocks = [w_ref[c, start : start + 128, :] for c in range(2)]
        parts = [p[:, 128 * c : 128 * c + 128] for c in range(2)]
        left = jnp.concatenate([nn(parts[c], blocks[c]) for c in range(2)], axis=1).astype(BF)
        plain[...] = nt(left, p).astype(BF)
        left = jnp.concatenate([nt(parts[c], blocks[c]) for c in range(2)], axis=1).astype(BF)
        flipped[...] = nt(left, p).astype(BF)
    lane = lax.broadcasted_iota(jnp.int32, (64, 128), 1)
    pairs = []
    for c in range(2):
        packed = w_ref[c, 256:320, :].astype(F32)
        pairs.append(
            jnp.concatenate(
                [jnp.where(lane < 64, packed, 0.0), jnp.where(lane < 64, 0.0, packed)], axis=0
            ).astype(BF)
        )
    parts = [q[:, 128 * c : 128 * c + 128] for c in range(2)]
    left = jnp.concatenate([nn(parts[c], pairs[c]) for c in range(2)], axis=1).astype(BF)
    l_ref[...] = nt(left, q).astype(BF)
    left = jnp.concatenate([nt(parts[c], pairs[c]) for c in range(2)], axis=1).astype(BF)
    lt_ref[...] = nt(left, q).astype(BF)


def turn_kernel(x_ref, o_ref):
    p = feature_order(256, 256)
    o_ref[...] = (nt(p[:, :128], x_ref[0]) + nt(p[:, 128:], x_ref[1])).astype(BF)


def first_kernel(x_ref, rt_ref, z_ref):
    put_rows(z_ref, nn(rt_ref[...], x_ref[...]))


def mix_kernel(z_ref, w_ref, u_ref):
    put_rows(u_ref, nn(w_ref[...], rows_of(z_ref).astype(BF)))


def gated_kernel(x_ref, u_ref, gt_ref, rt_ref, x_out, z_ref):
    x = x_ref[...]
    sig = jax.nn.sigmoid(nn(gt_ref[...], x))
    new = (x.astype(F32) + rows_of(u_ref) * sig).astype(BF)
    x_out[...] = new
    put_rows(z_ref, nn(rt_ref[...], new))


def gate_back(upper, x, u, gt, gu_ref, gg_ref):
    sig = jax.nn.sigmoid(nn(gt, x))
    put_rows(gu_ref, upper * sig)
    gg_ref[...] = (upper * u * sig * (1.0 - sig)).astype(BF)


def back_start_kernel(y_ref, x_ref, u_ref, gt_ref, gu_ref, gg_ref):
    gate_back(y_ref[...].astype(F32), x_ref[...], rows_of(u_ref), gt_ref[...], gu_ref, gg_ref)


def lower_of(y_ref, gz_ref, gg_ref, r_ref, g_ref):
    gz = rows_of(gz_ref).astype(BF)
    lower = y_ref[...].astype(F32) + nn(r_ref[...], gz)
    return (lower + nn(g_ref[...], gg_ref[...])).astype(BF)


def back_kernel(y_ref, gz_ref, gg_ref, r_ref, g_ref, x_ref, u_ref, gt_ref, y_out, gu_ref, gg_out):
    lower = lower_of(y_ref, gz_ref, gg_ref, r_ref, g_ref)
    y_out[...] = lower
    gate_back(lower.astype(F32), x_ref[...], rows_of(u_ref), gt_ref[...], gu_ref, gg_out)


def back_end_kernel(y_ref, gz_ref, gg_ref, r_ref, g_ref, y_out):
    y_out[...] = lower_of(y_ref, gz_ref, gg_ref, r_ref, g_ref)


def grads_kernel(*refs):
    ins, (w_out, y_out) = refs[:-2], refs[-2:]
    pt = feature_order(256, 256, True)
    qt = position_order(256, 256, True)
    r_sum = g_sum = l_sum = None
    n = ins[0].shape[-1]
    for c in range(CHUNKS):
        x, gz, gg, z, gu, y = ins[6 * c : 6 * c + 6]
        x_n = nn(pt, x[...]).astype(BF)
        gz_n = nn(pt, rows_of(gz).astype(BF)).astype(BF)
        gg_n = nn(pt, gg[...]).astype(BF)
        z_n = nn(qt, rows_of(z).astype(BF)).astype(BF)
        gu_n = nn(qt, rows_of(gu).astype(BF)).astype(BF)
        y_n = nn(pt, y[...])
        r_c = [nt(x_n[128 * i : 128 * i + 128], gz_n[128 * i : 128 * i + 128]) for i in range(2)]
        g_c = [nt(x_n[128 * i : 128 * i + 128], gg_n[128 * i : 128 * i + 128]) for i in range(2)]
        l_c = [nt(z_n[128 * i : 128 * i + 128], gu_n[128 * i : 128 * i + 128]) for i in range(2)]
        if r_sum is None:
            r_sum, g_sum, l_sum = r_c, g_c, l_c
        else:
            r_sum = [a + b for a, b in zip(r_sum, r_c)]
            g_sum = [a + b for a, b in zip(g_sum, g_c)]
            l_sum = [a + b for a, b in zip(l_sum, l_c)]
        for i in range(2):
            y_out[i, n * c : n * c + n, :] = y_n[128 * i : 128 * i + 128].T.astype(BF)
    lane = lax.broadcasted_iota(jnp.int32, (64, 128), 1)
    for i in range(2):
        w_out[i, 0:128, :] = r_sum[i].astype(w_out.dtype)
        w_out[i, 128:256, :] = g_sum[i].astype(w_out.dtype)
        w_out[i, 256:320, :] = jnp.where(lane < 64, l_sum[i][:64], l_sum[i][64:]).astype(w_out.dtype)


def run(kernel, outs, *args, dots=1):
    n = args[0].shape[-1]
    nbytes = sum(a.size * a.dtype.itemsize for a in args)
    return pl.pallas_call(
        kernel,
        out_shape=outs,
        compiler_params=pltpu.CompilerParams(vmem_limit_bytes=16 << 20),
        cost_estimate=pl.CostEstimate(
            flops=dots * 2 * 256 * 256 * n, bytes_accessed=2 * nbytes, transcendentals=0
        ),
    )(*args)


def sds(*shape, dtype=BF):
    return jax.ShapeDtypeStruct(shape, dtype)


def shards(inputs, cotangent, r_weight, g_weight, l_weight):
    layers = r_weight.shape[0] * lax.axis_size("x")
    tokens = inputs.shape[0] // (lax.axis_size("x") * 2)
    n = tokens // CHUNKS
    sect = lax.axis_index("x")
    core = lax.axis_index("c")

    l_flat = jnp.concatenate([l_weight[0, 0], l_weight[0, 1]], axis=1)
    packed = jnp.concatenate([r_weight[0, 0], g_weight[0, 0], l_flat], axis=0)
    every = lax.all_gather(packed, ("x", "c"), axis=0, tiled=False)
    every = every.reshape(layers, 2, 320, 128)
    mats = [run(prepare_kernel, [sds(256, 256)] * 6, every[s]) for s in range(layers)]

    def own_part(whole):
        mine = lax.dynamic_slice_in_dim(whole, (sect * 2 + core) * tokens, tokens, 0)
        other = lax.dynamic_slice_in_dim(whole, (sect * 2 + 1 - core) * tokens, tokens, 0)
        other = lax.ppermute(other, "c", [(0, 1), (1, 0)])
        low = jnp.where(core == 0, mine, other)
        high = jnp.where(core == 0, other, mine)
        pair = jnp.stack([low, high])
        return [run(turn_kernel, sds(256, n), pair[:, i * n : i * n + n]) for i in range(CHUNKS)]

    def swap(block):
        return lax.all_to_all(block, ("y", "z"), 0, 0, tiled=True)

    flat = sds(256, n)
    sent = sds(32, 8, n)
    ids = range(CHUNKS)
    x = [own_part(inputs)]
    y = own_part(cotangent)
    z_all, u_all = [], []
    z = [run(first_kernel, sent, x[0][i], mats[0][1]) for i in ids]
    for s in range(layers):
        z = [swap(z[i]) for i in ids]
        z_all.append(z)
        u = [swap(run(mix_kernel, sent, z[i], mats[s][5])) for i in ids]
        u_all.append(u)
        if s + 1 < layers:
            both = [
                run(gated_kernel, [flat, sent], x[s][i], u[i], mats[s][3], mats[s + 1][1], dots=2)
                for i in ids
            ]
            x.append([b[0] for b in both])
            z = [b[1] for b in both]
    last = layers - 1
    both = [
        run(back_start_kernel, [sent, flat], y[i], x[last][i], u_all[last][i], mats[last][3])
        for i in ids
    ]
    gu = [b[0] for b in both]
    gg = [b[1] for b in both]
    w_parts, y_parts = [], []
    for s in range(last, -1, -1):
        gu = [swap(gu[i]) for i in ids]
        gz = [swap(run(mix_kernel, sent, gu[i], mats[s][4])) for i in ids]
        held = (x[s], gz, gg, z_all[s], gu)
        if s > 0:
            trio = [
                run(
                    back_kernel,
                    [flat, sent, flat],
                    y[i],
                    gz[i],
                    gg[i],
                    mats[s][0],
                    mats[s][2],
                    x[s - 1][i],
                    u_all[s - 1][i],
                    mats[s - 1][3],
                    dots=3,
                )
                for i in ids
            ]
            y = [t[0] for t in trio]
            gu = [t[1] for t in trio]
            gg = [t[2] for t in trio]
        else:
            y = [
                run(back_end_kernel, flat, y[i], gz[i], gg[i], mats[s][0], mats[s][2], dots=2)
                for i in ids
            ]
        args = []
        for i in ids:
            args += [a[i] for a in held] + [y[i]]
        w_part, y_part = run(
            grads_kernel, [sds(2, 320, 128), sds(2, tokens, 128)], *args, dots=12
        )
        w_parts.insert(0, w_part)
        y_parts.insert(0, y_part)

    w_sent = jnp.stack(w_parts).reshape(layers * 2, 320, 128)
    y_sent = jnp.stack(y_parts).reshape(layers * 2, tokens, 128)
    y_back = lax.all_to_all(y_sent, ("x", "c"), 0, 0, tiled=True)
    w_back = lax.all_to_all(w_sent, ("x", "c"), 0, 0, tiled=True)
    total = jnp.sum(w_back.astype(F32), axis=0)
    r_grad, g_grad, l_flat = total[:128], total[128:256], total[256:]
    l_grad = jnp.stack([l_flat[:, :64], l_flat[:, 64:]])
    return (
        y_back.reshape(1, layers * 2 * tokens, 128),
        r_grad[None, None],
        g_grad[None, None],
        l_grad[None],
    )


def solution(mesh):
    grid = Mesh(mesh.devices.reshape(4, 4, 8, 2), ("x", "y", "z", "c"))
    blk = ("y", "z", "c")
    return jax.shard_map(
        shards,
        mesh=grid,
        in_specs=(
            P(None, blk),
            P(None, blk),
            P("x", blk, None, None),
            P("x", blk, None, None),
            P("x", blk, None, None),
        ),
        out_specs=(
            P("x", None, blk),
            P("x", blk, None, None),
            P("x", blk, None, None),
            P("x", blk, None, None),
        ),
        check_vma=False,
    )
```

time: 1240 us -> 543 us (0.44); the launches traced: 1220 us -> 540 us
  local copies, waits for them, and re-layouts: 268 us -> 62.1 us
  other arithmetic: 136 us -> 7.13 us
  blocking collectives: 127 us -> 13.6 us
  matrix products: 111 us -> 0 us
  starting transfers between devices: 278 us -> 193 us
  waiting for transfers between devices: 298 us -> 234 us
  Pallas kernels: 0 us -> 28.4 us
    all_to_all x8 -> x0, blocking collectives: 127 us -> none  [the longest x6 95.8 us: layer_forward(): lax.all_to_all(first, 'blk', split_axis=2, concat_axis=1, tiled=True)]
    dot_general x99 -> x0, matrix products: 111 us -> none  [the longest x11 20.1 us: layer_backward(): jnp.einsum('nbk,bjk->nbj', grad_gate, g_w, preferred_element_type=jnp.flo...]
    all_to_all x63 -> x0, local copies, waits for them, and re-layouts: 92.9 us -> none  [the longest x31 38.5 us: layer_forward(): lax.all_to_all(first, 'blk', split_axis=2, concat_axis=1, tiled=True)]
    unnamed x22 -> x0, other arithmetic: 57.9 us -> none
    ppermute x20 -> x2, starting transfers between devices: 58.6 us -> 3.4 us  [own_part(): other = lax.ppermute(other, 'c', [(0, 1), (1, 0)])]
    convert_element_type x54 -> x0, local copies, waits for them, and re-layouts: 54.3 us -> none  [the longest x10 14.8 us: layer_forward(): mixed.astype(jnp.float32) * jax.nn.sigmoid(gate)]
    dynamic_update_slice x31 -> x0, other arithmetic: 38.9 us -> none  [keep_slot(): lax.dynamic_update_index_in_dim(buffer, jnp.where(valid, value, older), p...]
    ppermute x20 -> x2, waiting for transfers between devices: 38.2 us -> 0.01 us  [own_part(): other = lax.ppermute(other, 'c', [(0, 1), (1, 0)])]
  transfers between devices with their start and end apart: 56 -> 36, of which waited for: 51 -> 33; matrix products, arithmetic and copies ran while one was open for 11% -> 1% of each run, Pallas kernels for 0% -> 5%
where the time goes in v1:
time: 543 us; the launch traced here: 540 us
  waiting for transfers between devices  234 us (43%)
  starting transfers between devices  193 us (36%)
  local copies, waits for them, and re-layouts  62.1 us (11%)
  Pallas kernels  28.4 us (5%)
  blocking collectives  13.6 us (3%)
  other arithmetic  7.13 us (1%)
    all_to_all x32, waiting for transfers between devices, swap(): return lax.all_to_all(block, ('y', 'z'), 0, 0, tiled=True)  211 us
    all_to_all x32, starting transfers between devices, swap(): return lax.all_to_all(block, ('y', 'z'), 0, 0, tiled=True)  149 us
    unnamed x229, local copies, waits for them, and re-layouts  58.8 us
    all_to_all x1, starting transfers between devices, shards(): w_back = lax.all_to_all(w_sent, ('x', 'c'), 0, 0, tiled=True)  36.4 us
    pallas_call x46, Pallas kernels, run(): pl.pallas_call(kernel, out_shape=outs, compiler_params=pltpu.CompilerPara...  28.4 us
    all_gather x1, blocking collectives, shards(): every = lax.all_gather(packed, ('x', 'c'), axis=0, tiled=False)  13.6 us
    all_to_all x1, waiting for transfers between devices, shards(): y_back = lax.all_to_all(y_sent, ('x', 'c'), 0, 0, tiled=True)  13.5 us
  transfers between devices with their start and end apart: 36, of which 33 were waited for; matrix products, arithmetic and copies ran while one was open for 1% of the time, Pallas kernels for 5%

profile of v1, /device:TPU:1, one launch (start us, length us, event | category | flops | bytes accessed | tf_op | source)
XLA Modules:
  0.0 540.0 jit_solution(9886433153511738931)
XLA Ops:
  1.6 3.3 collective-permute-start.1
  7.5 13.6 %all-gather = bf16[2560,128]{1,0:T(8,128)(2,1)S(1)} all-gather(bf16[320,128]{1,0:T(8,128)(2,1)S(1)} %maximum_maximum_fusion), channel_id=2, replica_groups=mesh['x'=4,'y'=4,'z'=8,'c'=2] {'x','c'}, dimensions={0}, use_global_device_ids=true | all-gather | bytes 737280 | tf_op jit(solution)/shard_map/all_gather | solution.py:177
  24.8 9.8 %all-to-all-start = ((bf16[32,8,256]{2,1,0:T(8,128)(2,1)}), bf16[32,8,256]{2,1,0:T(8,128)(2,1)S(1)}, u32[]{:S(2)}, u32[]{:S(2)}) async-start(bf16[32,8,256]{2,1,0:T(8,128)(2,1)} %shard_map.87), calls=%async_computation | async-start | bytes 262144 | tf_op jit(solution)/shard_map/all_to_all | solution.py:191
  35.7 8.1 %all-to-all-done.z_ref.refs_3_ = bf16[32,8,256]{2,1,0:T(8,128)(2,1)S(1)} async-done(((bf16[32,8,256]{2,1,0:T(8,128)(2,1)}), bf16[32,8,256]{2,1,0:T(8,128)(2,1)S(1)}, u32[]{:S(2)}, u32[]{:S(2)}) %all-to-all-start) | async-done | bytes 131104 | tf_op jit(solution)/shard_map/all_to_all | solution.py:191
  43.8 4.4 all-to-all-start.16
  49.1 8.3 %all-to-all-done.16.z_ref.refs_9_ = bf16[32,8,256]{2,1,0:T(8,128)(2,1)S(1)} async-done(((bf16[32,8,256]{2,1,0:T(8,128)(2,1)}), bf16[32,8,256]{2,1,0:T(8,128)(2,1)S(1)}, u32[]{:S(2)}, u32[]{:S(2)}) %all-to-all-start.16) | async-done | bytes 131104 | tf_op jit(solution)/shard_map/all_to_all | solution.py:191
  57.4 3.8 all-to-all-start.1
  62.1 8.3 %all-to-all-done.1.u_ref = bf16[32,8,256]{2,1,0:T(8,128)(2,1)S(1)} async-done(((bf16[32,8,256]{2,1,0:T(8,128)(2,1)}), bf16[32,8,256]{2,1,0:T(8,128)(2,1)S(1)}, u32[]{:S(2)}, u32[]{:S(2)}) %all-to-all-start.1) | async-done | bytes 131104 | tf_op jit(solution)/shard_map/all_to_all | solution.py:191
  70.4 3.9 all-to-all-start.17
  76.0 7.4 %all-to-all-done.17.u_ref = bf16[32,8,256]{2,1,0:T(8,128)(2,1)S(1)} async-done(((bf16[32,8,256]{2,1,0:T(8,128)(2,1)}), bf16[32,8,256]{2,1,0:T(8,128)(2,1)S(1)}, u32[]{:S(2)}, u32[]{:S(2)}) %all-to-all-start.17) | async-done | bytes 131104 | tf_op jit(solution)/shard_map/all_to_all | solution.py:191
  83.4 3.8 all-to-all-start.2
  88.3 8.1 %all-to-all-done.2.z_ref.refs_3_ = bf16[32,8,256]{2,1,0:T(8,128)(2,1)S(1)} async-done(((bf16[32,8,256]{2,1,0:T(8,128)(2,1)}), bf16[32,8,256]{2,1,0:T(8,128)(2,1)S(1)}, u32[]{:S(2)}, u32[]{:S(2)}) %all-to-all-start.2) | async-done | bytes 131104 | tf_op jit(solution)/shard_map/all_to_all | solution.py:191
  96.4 3.8 all-to-all-start.18
  101.1 8.3 %all-to-all-done.18.z_ref.refs_9_ = bf16[32,8,256]{2,1,0:T(8,128)(2,1)S(1)} async-done(((bf16[32,8,256]{2,1,0:T(8,128)(2,1)}), bf16[32,8,256]{2,1,0:T(8,128)(2,1)S(1)}, u32[]{:S(2)}, u32[]{:S(2)}) %all-to-all-start.18) | async-done | bytes 131104 | tf_op jit(solution)/shard_map/all_to_all | solution.py:191
  109.4 3.8 all-to-all-start.3
  114.1 8.3 %all-to-all-done.3.u_ref = bf16[32,8,256]{2,1,0:T(8,128)(2,1)S(1)} async-done(((bf16[32,8,256]{2,1,0:T(8,128)(2,1)}), bf16[32,8,256]{2,1,0:T(8,128)(2,1)S(1)}, u32[]{:S(2)}, u32[]{:S(2)}) %all-to-all-start.3) | async-done | bytes 131104 | tf_op jit(solution)/shard_map/all_to_all | solution.py:191
  122.4 3.8 all-to-all-start.19
  129.3 6.1 %all-to-all-done.19.u_ref = bf16[32,8,256]{2,1,0:T(8,128)(2,1)S(1)} async-done(((bf16[32,8,256]{2,1,0:T(8,128)(2,1)}), bf16[32,8,256]{2,1,0:T(8,128)(2,1)S(1)}, u32[]{:S(2)}, u32[]{:S(2)}) %all-to-all-start.19) | async-done | bytes 131104 | tf_op jit(solution)/shard_map/all_to_all | solution.py:191
  135.4 3.8 all-to-all-start.4
  140.3 8.1 %all-to-all-done.4.z_ref.refs_3_ = bf16[32,8,256]{2,1,0:T(8,128)(2,1)S(1)} async-done(((bf16[32,8,256]{2,1,0:T(8,128)(2,1)}), bf16[32,8,256]{2,1,0:T(8,128)(2,1)S(1)}, u32[]{:S(2)}, u32[]{:S(2)}) %all-to-all-start.4) | async-done | bytes 131104 | tf_op jit(solution)/shard_map/all_to_all | solution.py:191
  148.4 3.8 all-to-all-start.20
  153.1 8.4 %all-to-all-done.20.z_ref.refs_9_ = bf16[32,8,256]{2,1,0:T(8,128)(2,1)S(1)} async-done(((bf16[32,8,256]{2,1,0:T(8,128)(2,1)}), bf16[32,8,256]{2,1,0:T(8,128)(2,1)S(1)}, u32[]{:S(2)}, u32[]{:S(2)}) %all-to-all-start.20) | async-done | bytes 131104 | tf_op jit(solution)/shard_map/all_to_all | solution.py:191
  161.5 3.8 all-to-all-start.5
  166.2 8.3 %all-to-all-done.5.u_ref = bf16[32,8,256]{2,1,0:T(8,128)(2,1)S(1)} async-done(((bf16[32,8,256]{2,1,0:T(8,128)(2,1)}), bf16[32,8,256]{2,1,0:T(8,128)(2,1)S(1)}, u32[]{:S(2)}, u32[]{:S(2)}) %all-to-all-start.5) | async-done | bytes 131104 | tf_op jit(solution)/shard_map/all_to_all | solution.py:191
  174.5 4.0 all-to-all-start.21
  182.2 6.1 %all-to-all-done.21.u_ref = bf16[32,8,256]{2,1,0:T(8,128)(2,1)S(1)} async-done(((bf16[32,8,256]{2,1,0:T(8,128)(2,1)}), bf16[32,8,256]{2,1,0:T(8,128)(2,1)S(1)}, u32[]{:S(2)}, u32[]{:S(2)}) %all-to-all-start.21) | async-done | bytes 131104 | tf_op jit(solution)/shard_map/all_to_all | solution.py:191
  188.3 3.8 all-to-all-start.6
  193.9 7.4 %all-to-all-done.6.z_ref.refs_3_ = bf16[32,8,256]{2,1,0:T(8,128)(2,1)S(1)} async-done(((bf16[32,8,256]{2,1,0:T(8,128)(2,1)}), bf16[32,8,256]{2,1,0:T(8,128)(2,1)S(1)}, u32[]{:S(2)}, u32[]{:S(2)}) %all-to-all-start.6) | async-done | bytes 131104 | tf_op jit(solution)/shard_map/all_to_all | solution.py:191
  201.3 4.4 all-to-all-start.22
  206.6 8.3 %all-to-all-done.22.z_ref.refs_9_ = bf16[32,8,256]{2,1,0:T(8,128)(2,1)S(1)} async-done(((bf16[32,8,256]{2,1,0:T(8,128)(2,1)}), bf16[32,8,256]{2,1,0:T(8,128)(2,1)S(1)}, u32[]{:S(2)}, u32[]{:S(2)}) %all-to-all-start.22) | async-done | bytes 131104 | tf_op jit(solution)/shard_map/all_to_all | solution.py:191
  214.9 3.8 all-to-all-start.7
  219.6 8.3 %all-to-all-done.7.u_ref = bf16[32,8,256]{2,1,0:T(8,128)(2,1)S(1)} async-done(((bf16[32,8,256]{2,1,0:T(8,128)(2,1)}), bf16[32,8,256]{2,1,0:T(8,128)(2,1)S(1)}, u32[]{:S(2)}, u32[]{:S(2)}) %all-to-all-start.7) | async-done | bytes 131104 | tf_op jit(solution)/shard_map/all_to_all | solution.py:191
  227.9 4.6 all-to-all-start.23
  241.6 5.9 %all-to-all-start.8 = ((bf16[32,8,256]{2,1,0:T(8,128)(2,1)}), bf16[32,8,256]{2,1,0:T(8,128)(2,1)S(1)}, u32[]{:S(2)}, u32[]{:S(2)}) async-start(bf16[32,8,256]{2,1,0:T(8,128)(2,1)} %copy-done.109), calls=%async_computation.8 | async-start | bytes 262144 | tf_op jit(solution)/shard_map/all_to_all | solution.py:191
  256.8 6.2 %all-to-all-start.24 = ((bf16[32,8,256]{2,1,0:T(8,128)(2,1)}), bf16[32,8,256]{2,1,0:T(8,128)(2,1)S(1)}, u32[]{:S(2)}, u32[]{:S(2)}) async-start(bf16[32,8,256]{2,1,0:T(8,128)(2,1)} %copy-done.113), calls=%async_computation.24 | async-start | bytes 262144 | tf_op jit(solution)/shard_map/all_to_all | solution.py:191
  263.8 8.3 %all-to-all-done.24.z_ref.refs_10_ = bf16[32,8,256]{2,1,0:T(8,128)(2,1)S(1)} async-done(((bf16[32,8,256]{2,1,0:T(8,128)(2,1)}), bf16[32,8,256]{2,1,0:T(8,128)(2,1)S(1)}, u32[]{:S(2)}, u32[]{:S(2)}) %all-to-all-start.24) | async-done | bytes 131104 | tf_op jit(solution)/shard_map/all_to_all | solution.py:191
  272.1 3.9 all-to-all-start.9
  276.8 8.3 %all-to-all-done.9.gz_ref.refs_1_ = bf16[32,8,256]{2,1,0:T(8,128)(2,1)S(1)} async-done(((bf16[32,8,256]{2,1,0:T(8,128)(2,1)}), bf16[32,8,256]{2,1,0:T(8,128)(2,1)S(1)}, u32[]{:S(2)}, u32[]{:S(2)}) %all-to-all-start.9) | async-done | bytes 131104 | tf_op jit(solution)/shard_map/all_to_all | solution.py:191
  285.1 3.8 all-to-all-start.25
  298.1 6.2 %all-to-all-start.10 = ((bf16[32,8,256]{2,1,0:T(8,128)(2,1)}), bf16[32,8,256]{2,1,0:T(8,128)(2,1)S(1)}, u32[]{:S(2)}, u32[]{:S(2)}) async-start(bf16[32,8,256]{2,1,0:T(8,128)(2,1)} %copy-done.106), calls=%async_computation.10 | async-start | bytes 262144 | tf_op jit(solution)/shard_map/all_to_all | solution.py:191
  313.4 6.0 %all-to-all-start.26 = ((bf16[32,8,256]{2,1,0:T(8,128)(2,1)}), bf16[32,8,256]{2,1,0:T(8,128)(2,1)S(1)}, u32[]{:S(2)}, u32[]{:S(2)}) async-start(bf16[32,8,256]{2,1,0:T(8,128)(2,1)} %copy-done.110), calls=%async_computation.26 | async-start | bytes 262144 | tf_op jit(solution)/shard_map/all_to_all | solution.py:191
  320.3 8.3 %all-to-all-done.26.z_ref.refs_10_ = bf16[32,8,256]{2,1,0:T(8,128)(2,1)S(1)} async-done(((bf16[32,8,256]{2,1,0:T(8,128)(2,1)}), bf16[32,8,256]{2,1,0:T(8,128)(2,1)S(1)}, u32[]{:S(2)}, u32[]{:S(2)}) %all-to-all-start.26) | async-done | bytes 131104 | tf_op jit(solution)/shard_map/all_to_all | solution.py:191
  328.6 3.9 all-to-all-start.11
  333.3 8.3 %all-to-all-done.11.gz_ref.refs_1_ = bf16[32,8,256]{2,1,0:T(8,128)(2,1)S(1)} async-done(((bf16[32,8,256]{2,1,0:T(8,128)(2,1)}), bf16[32,8,256]{2,1,0:T(8,128)(2,1)S(1)}, u32[]{:S(2)}, u32[]{:S(2)}) %all-to-all-start.11) | async-done | bytes 131104 | tf_op jit(solution)/shard_map/all_to_all | solution.py:191
  341.6 3.8 all-to-all-start.27
  351.4 3.3 all-to-all-done.27.gz_ref.refs_7_
  354.7 6.0 %all-to-all-start.12 = ((bf16[32,8,256]{2,1,0:T(8,128)(2,1)}), bf16[32,8,256]{2,1,0:T(8,128)(2,1)S(1)}, u32[]{:S(2)}, u32[]{:S(2)}) async-start(bf16[32,8,256]{2,1,0:T(8,128)(2,1)} %copy-done.107), calls=%async_computation.12 | async-start | bytes 262144 | tf_op jit(solution)/shard_map/all_to_all | solution.py:191
  369.9 6.0 %all-to-all-start.28 = ((bf16[32,8,256]{2,1,0:T(8,128)(2,1)}), bf16[32,8,256]{2,1,0:T(8,128)(2,1)S(1)}, u32[]{:S(2)}, u32[]{:S(2)}) async-start(bf16[32,8,256]{2,1,0:T(8,128)(2,1)} %copy-done.111), calls=%async_computation.28 | async-start | bytes 262144 | tf_op jit(solution)/shard_map/all_to_all | solution.py:191
  376.7 8.3 %all-to-all-done.28.z_ref.refs_10_ = bf16[32,8,256]{2,1,0:T(8,128)(2,1)S(1)} async-done(((bf16[32,8,256]{2,1,0:T(8,128)(2,1)}), bf16[32,8,256]{2,1,0:T(8,128)(2,1)S(1)}, u32[]{:S(2)}, u32[]{:S(2)}) %all-to-all-start.28) | async-done | bytes 131104 | tf_op jit(solution)/shard_map/all_to_all | solution.py:191
  385.0 3.8 all-to-all-start.13
  389.7 8.4 %all-to-all-done.13.gz_ref.refs_1_ = bf16[32,8,256]{2,1,0:T(8,128)(2,1)S(1)} async-done(((bf16[32,8,256]{2,1,0:T(8,128)(2,1)}), bf16[32,8,256]{2,1,0:T(8,128)(2,1)S(1)}, u32[]{:S(2)}, u32[]{:S(2)}) %all-to-all-start.13) | async-done | bytes 131104 | tf_op jit(solution)/shard_map/all_to_all | solution.py:191
  398.2 3.8 all-to-all-start.29
  408.0 3.3 all-to-all-done.29.gz_ref.refs_7_
  411.3 6.2 %all-to-all-start.14 = ((bf16[32,8,256]{2,1,0:T(8,128)(2,1)}), bf16[32,8,256]{2,1,0:T(8,128)(2,1)S(1)}, u32[]{:S(2)}, u32[]{:S(2)}) async-start(bf16[32,8,256]{2,1,0:T(8,128)(2,1)} %copy-done.108), calls=%async_computation.14 | async-start | bytes 262144 | tf_op jit(solution)/shard_map/all_to_all | solution.py:191
  423.4 3.3 all-to-all-done.14.z_ref.refs_4_
  426.8 5.7 %all-to-all-start.30 = ((bf16[32,8,256]{2,1,0:T(8,128)(2,1)}), bf16[32,8,256]{2,1,0:T(8,128)(2,1)S(1)}, u32[]{:S(2)}, u32[]{:S(2)}) async-start(bf16[32,8,256]{2,1,0:T(8,128)(2,1)} %copy-done.112), calls=%async_computation.30 | async-start | bytes 262144 | tf_op jit(solution)/shard_map/all_to_all | solution.py:191
  433.3 8.6 %all-to-all-done.30.z_ref.refs_10_ = bf16[32,8,256]{2,1,0:T(8,128)(2,1)S(1)} async-done(((bf16[32,8,256]{2,1,0:T(8,128)(2,1)}), bf16[32,8,256]{2,1,0:T(8,128)(2,1)S(1)}, u32[]{:S(2)}, u32[]{:S(2)}) %all-to-all-start.30) | async-done | bytes 131104 | tf_op jit(solution)/shard_map/all_to_all | solution.py:191
  442.0 4.4 all-to-all-start.15
  447.3 8.4 %all-to-all-done.15.gz_ref.refs_1_ = bf16[32,8,256]{2,1,0:T(8,128)(2,1)S(1)} async-done(((bf16[32,8,256]{2,1,0:T(8,128)(2,1)}), bf16[32,8,256]{2,1,0:T(8,128)(2,1)S(1)}, u32[]{:S(2)}, u32[]{:S(2)}) %all-to-all-start.15) | async-done | bytes 131104 | tf_op jit(solution)/shard_map/all_to_all | solution.py:191
  455.7 3.8 all-to-all-start.31
  472.5 36.4 %all-to-all-start.33 = ((bf16[8,320,128]{2,1,0:T(8,128)(2,1)}), bf16[8,320,128]{2,1,0:T(8,128)(2,1)S(1)}, u32[]{:S(2)}, u32[]{:S(2)}) async-start(bf16[8,320,128]{2,1,0:T(8,128)(2,1)} %bitcast.53), calls=%async_computation.33 | async-start | bytes 1310720 | tf_op jit(solution)/shard_map/all_to_all | solution.py:261
  510.0 9.6 %all-to-all-done.33 = bf16[8,320,128]{2,1,0:T(8,128)(2,1)S(1)} async-done(((bf16[8,320,128]{2,1,0:T(8,128)(2,1)}), bf16[8,320,128]{2,1,0:T(8,128)(2,1)S(1)}, u32[]{:S(2)}, u32[]{:S(2)}) %all-to-all-start.33) | async-done | bytes 655392 | tf_op jit(solution)/shard_map/all_to_all | solution.py:261
  519.6 4.4 all-to-all-start.32
  525.5 13.5 %all-to-all-done.32 = bf16[8,512,128]{2,1,0:T(8,128)(2,1)S(1)} async-done(((bf16[8,512,128]{2,1,0:T(8,128)(2,1)}), bf16[8,512,128]{2,1,0:T(8,128)(2,1)S(1)}, u32[]{:S(2)}, u32[]{:S(2)}) %all-to-all-start.32) | async-done | bytes 1048608 | tf_op jit(solution)/shard_map/all_to_all | solution.py:260
  (298 shorter events, 113.6 us)
Async XLA Ops:
  1.6 20.2 %collective-permute-start.1 = (bf16[512,128]{1,0:T(8,128)(2,1)S(1)}, bf16[512,128]{1,0:T(8,128)(2,1)S(1)}, u32[]{:S(2)}, u32[]{:S(2)}) collective-permute-start(bf16[512,128]{1,0:T(8,128)(2,1)S(1)} %constant_dynamic-slice_fusion), channel_id=1, source_target_pairs={{0,1},{1,0},{2,3},{3,2},{4,5},{5,4},{6,7},{7,6},{8,9},{9,8},{10,11... | collective-permute-start | bytes 393224 | tf_op jit(solution)/shard_map/ppermute | solution.py:184
  5.8 16.0 %collective-permute-start = (bf16[512,128]{1,0:T(8,128)(2,1)S(1)}, bf16[512,128]{1,0:T(8,128)(2,1)S(1)}, u32[]{:S(2)}, u32[]{:S(2)}) collective-permute-start(bf16[512,128]{1,0:T(8,128)(2,1)S(1)} %constant_dynamic-slice_fusion.1), channel_id=1, source_target_pairs={{0,1},{1,0},{2,3},{3,2},{4,5},{5,4},{6,7},{7,6},{8,9},{9,8},{10,11... | collective-permute-start | bytes 393224 | tf_op jit(solution)/shard_map/ppermute | solution.py:184
  21.7 1.9 copy-start.41
  21.8 1.9 copy-start.10
  21.8 3.0 copy-start.43
  24.8 19.0 %all-to-all-start = ((bf16[32,8,256]{2,1,0:T(8,128)(2,1)}), bf16[32,8,256]{2,1,0:T(8,128)(2,1)S(1)}, u32[]{:S(2)}, u32[]{:S(2)}) async-start(bf16[32,8,256]{2,1,0:T(8,128)(2,1)} %shard_map.87), calls=%async_computation | async-start | bytes 262144 | tf_op jit(solution)/shard_map/all_to_all | solution.py:191
  43.8 13.6 %all-to-all-start.16 = ((bf16[32,8,256]{2,1,0:T(8,128)(2,1)}), bf16[32,8,256]{2,1,0:T(8,128)(2,1)S(1)}, u32[]{:S(2)}, u32[]{:S(2)}) async-start(bf16[32,8,256]{2,1,0:T(8,128)(2,1)} %shard_map.109), calls=%async_computation.16 | async-start | bytes 262144 | tf_op jit(solution)/shard_map/all_to_all | solution.py:191
  57.4 13.0 %all-to-all-start.1 = ((bf16[32,8,256]{2,1,0:T(8,128)(2,1)}), bf16[32,8,256]{2,1,0:T(8,128)(2,1)S(1)}, u32[]{:S(2)}, u32[]{:S(2)}) async-start(bf16[32,8,256]{2,1,0:T(8,128)(2,1)} %shard_map.88), calls=%async_computation.1 | async-start | bytes 262144 | tf_op jit(solution)/shard_map/all_to_all | solution.py:191
  70.4 13.0 %all-to-all-start.17 = ((bf16[32,8,256]{2,1,0:T(8,128)(2,1)}), bf16[32,8,256]{2,1,0:T(8,128)(2,1)S(1)}, u32[]{:S(2)}, u32[]{:S(2)}) async-start(bf16[32,8,256]{2,1,0:T(8,128)(2,1)} %shard_map.110), calls=%async_computation.17 | async-start | bytes 262144 | tf_op jit(solution)/shard_map/all_to_all | solution.py:191
  74.9 8.5 %copy-start.78 = (bf16[256,256]{1,0:T(8,128)(2,1)}, bf16[256,256]{1,0:T(8,128)(2,1)S(1)}, u32[]{:S(2)}) copy-start(bf16[256,256]{1,0:T(8,128)(2,1)S(1)} %get-tuple-element.103.r_ref) | copy-start | bytes 393220
  74.9 8.5 %copy-start.81 = (bf16[256,256]{1,0:T(8,128)(2,1)}, bf16[256,256]{1,0:T(8,128)(2,1)S(1)}, u32[]{:S(2)}) copy-start(bf16[256,256]{1,0:T(8,128)(2,1)S(1)} %get-tuple-element.104.g_ref) | copy-start | bytes 393220
  75.0 34.4 %copy-start.12 = (bf16[256,256]{1,0:T(8,128)(2,1)}, bf16[256,256]{1,0:T(8,128)(2,1)S(1)}, u32[]{:S(2)}) copy-start(bf16[256,256]{1,0:T(8,128)(2,1)S(1)} %get-tuple-element.101.w_ref) | copy-start | bytes 393220
  83.4 13.0 %all-to-all-start.2 = ((bf16[32,8,256]{2,1,0:T(8,128)(2,1)}), bf16[32,8,256]{2,1,0:T(8,128)(2,1)S(1)}, u32[]{:S(2)}, u32[]{:S(2)}) async-start(bf16[32,8,256]{2,1,0:T(8,128)(2,1)} %get-tuple-element.75), calls=%async_computation.2 | async-start | bytes 262144 | tf_op jit(solution)/shard_map/all_to_all | solution.py:191
  88.3 272.4 %copy-start = (bf16[256,256]{1,0:T(8,128)(2,1)}, bf16[256,256]{1,0:T(8,128)(2,1)S(1)}, u32[]{:S(2)}) copy-start(bf16[256,256]{1,0:T(8,128)(2,1)S(1)} %get-tuple-element.111.x_ref.refs_6_) | copy-start | bytes 393220
  96.4 13.0 %all-to-all-start.18 = ((bf16[32,8,256]{2,1,0:T(8,128)(2,1)}), bf16[32,8,256]{2,1,0:T(8,128)(2,1)S(1)}, u32[]{:S(2)}, u32[]{:S(2)}) async-start(bf16[32,8,256]{2,1,0:T(8,128)(2,1)} %get-tuple-element.112), calls=%async_computation.18 | async-start | bytes 262144 | tf_op jit(solution)/shard_map/all_to_all | solution.py:191
  109.4 13.0 %all-to-all-start.3 = ((bf16[32,8,256]{2,1,0:T(8,128)(2,1)}), bf16[32,8,256]{2,1,0:T(8,128)(2,1)S(1)}, u32[]{:S(2)}, u32[]{:S(2)}) async-start(bf16[32,8,256]{2,1,0:T(8,128)(2,1)} %shard_map.91), calls=%async_computation.3 | async-start | bytes 262144 | tf_op jit(solution)/shard_map/all_to_all | solution.py:191
  122.4 13.0 %all-to-all-start.19 = ((bf16[32,8,256]{2,1,0:T(8,128)(2,1)}), bf16[32,8,256]{2,1,0:T(8,128)(2,1)S(1)}, u32[]{:S(2)}, u32[]{:S(2)}) async-start(bf16[32,8,256]{2,1,0:T(8,128)(2,1)} %shard_map.112), calls=%async_computation.19 | async-start | bytes 262144 | tf_op jit(solution)/shard_map/all_to_all | solution.py:191
  128.2 7.2 %copy-start.84 = (bf16[256,256]{1,0:T(8,128)(2,1)}, bf16[256,256]{1,0:T(8,128)(2,1)S(1)}, u32[]{:S(2)}) copy-start(bf16[256,256]{1,0:T(8,128)(2,1)S(1)} %get-tuple-element.97.r_ref) | copy-start | bytes 393220
  129.3 159.6 %copy-start.2 = (bf16[256,256]{1,0:T(8,128)(2,1)}, bf16[256,256]{1,0:T(8,128)(2,1)S(1)}, u32[]{:S(2)}) copy-start(bf16[256,256]{1,0:T(8,128)(2,1)S(1)} %get-tuple-element.79.x_ref.refs_0_) | copy-start | bytes 393220
  135.4 13.0 %all-to-all-start.4 = ((bf16[32,8,256]{2,1,0:T(8,128)(2,1)}), bf16[32,8,256]{2,1,0:T(8,128)(2,1)S(1)}, u32[]{:S(2)}, u32[]{:S(2)}) async-start(bf16[32,8,256]{2,1,0:T(8,128)(2,1)} %get-tuple-element.80), calls=%async_computation.4 | async-start | bytes 262144 | tf_op jit(solution)/shard_map/all_to_all | solution.py:191
  140.3 163.9 %copy-start.4 = (bf16[256,256]{1,0:T(8,128)(2,1)}, bf16[256,256]{1,0:T(8,128)(2,1)S(1)}, u32[]{:S(2)}) copy-start(bf16[256,256]{1,0:T(8,128)(2,1)S(1)} %get-tuple-element.113.x_ref.refs_6_) | copy-start | bytes 393220
  148.4 13.1 %all-to-all-start.20 = ((bf16[32,8,256]{2,1,0:T(8,128)(2,1)}), bf16[32,8,256]{2,1,0:T(8,128)(2,1)S(1)}, u32[]{:S(2)}, u32[]{:S(2)}) async-start(bf16[32,8,256]{2,1,0:T(8,128)(2,1)} %get-tuple-element.114), calls=%async_computation.20 | async-start | bytes 262144 | tf_op jit(solution)/shard_map/all_to_all | solution.py:191
  161.5 13.0 %all-to-all-start.5 = ((bf16[32,8,256]{2,1,0:T(8,128)(2,1)}), bf16[32,8,256]{2,1,0:T(8,128)(2,1)S(1)}, u32[]{:S(2)}, u32[]{:S(2)}) async-start(bf16[32,8,256]{2,1,0:T(8,128)(2,1)} %shard_map.94), calls=%async_computation.5 | async-start | bytes 262144 | tf_op jit(solution)/shard_map/all_to_all | solution.py:191
  174.5 13.9 %all-to-all-start.21 = ((bf16[32,8,256]{2,1,0:T(8,128)(2,1)}), bf16[32,8,256]{2,1,0:T(8,128)(2,1)S(1)}, u32[]{:S(2)}, u32[]{:S(2)}) async-start(bf16[32,8,256]{2,1,0:T(8,128)(2,1)} %shard_map.114), calls=%async_computation.21 | async-start | bytes 262144 | tf_op jit(solution)/shard_map/all_to_all | solution.py:191
  181.2 7.2 %copy-start.90 = (bf16[256,256]{1,0:T(8,128)(2,1)}, bf16[256,256]{1,0:T(8,128)(2,1)S(1)}, u32[]{:S(2)}) copy-start(bf16[256,256]{1,0:T(8,128)(2,1)S(1)} %get-tuple-element.91.r_ref) | copy-start | bytes 393220
  182.2 52.1 %copy-start.24 = (bf16[256,256]{1,0:T(8,128)(2,1)}, bf16[256,256]{1,0:T(8,128)(2,1)S(1)}, u32[]{:S(2)}) copy-start(bf16[256,256]{1,0:T(8,128)(2,1)S(1)} %get-tuple-element.84.x_ref.refs_0_) | copy-start | bytes 393220
  188.3 13.0 %all-to-all-start.6 = ((bf16[32,8,256]{2,1,0:T(8,128)(2,1)}), bf16[32,8,256]{2,1,0:T(8,128)(2,1)S(1)}, u32[]{:S(2)}, u32[]{:S(2)}) async-start(bf16[32,8,256]{2,1,0:T(8,128)(2,1)} %get-tuple-element.85), calls=%async_computation.6 | async-start | bytes 262144 | tf_op jit(solution)/shard_map/all_to_all | solution.py:191
  201.3 13.6 %all-to-all-start.22 = ((bf16[32,8,256]{2,1,0:T(8,128)(2,1)}), bf16[32,8,256]{2,1,0:T(8,128)(2,1)S(1)}, u32[]{:S(2)}, u32[]{:S(2)}) async-start(bf16[32,8,256]{2,1,0:T(8,128)(2,1)} %get-tuple-element.116), calls=%async_computation.22 | async-start | bytes 262144 | tf_op jit(solution)/shard_map/all_to_all | solution.py:191
  214.9 13.0 %all-to-all-start.7 = ((bf16[32,8,256]{2,1,0:T(8,128)(2,1)}), bf16[32,8,256]{2,1,0:T(8,128)(2,1)S(1)}, u32[]{:S(2)}, u32[]{:S(2)}) async-start(bf16[32,8,256]{2,1,0:T(8,128)(2,1)} %shard_map.97), calls=%async_computation.7 | async-start | bytes 262144 | tf_op jit(solution)/shard_map/all_to_all | solution.py:191
  227.9 6.2 %copy-start.38 = (bf16[32,8,256]{2,1,0:T(8,128)(2,1)}, bf16[32,8,256]{2,1,0:T(8,128)(2,1)S(1)}, u32[]{:S(2)}) copy-start(bf16[32,8,256]{2,1,0:T(8,128)(2,1)S(1)} %all-to-all-done.7.u_ref) | copy-start | bytes 393220
  227.9 13.7 %all-to-all-start.23 = ((bf16[32,8,256]{2,1,0:T(8,128)(2,1)}), bf16[32,8,256]{2,1,0:T(8,128)(2,1)}, u32[]{:S(2)}, u32[]{:S(2)}) async-start(bf16[32,8,256]{2,1,0:T(8,128)(2,1)} %shard_map.116), calls=%async_computation.23 | async-start | bytes 262144 | tf_op jit(solution)/shard_map/all_to_all | solution.py:191
  234.1 28.8 %copy-start.17 = (bf16[256,256]{1,0:T(8,128)(2,1)S(1)}, bf16[256,256]{1,0:T(8,128)(2,1)}, u32[]{:S(2)}) copy-start(bf16[256,256]{1,0:T(8,128)(2,1)} %copy-done.16) | copy-start | bytes 393220
  241.6 15.1 %all-to-all-start.8 = ((bf16[32,8,256]{2,1,0:T(8,128)(2,1)}), bf16[32,8,256]{2,1,0:T(8,128)(2,1)S(1)}, u32[]{:S(2)}, u32[]{:S(2)}) async-start(bf16[32,8,256]{2,1,0:T(8,128)(2,1)} %copy-done.109), calls=%async_computation.8 | async-start | bytes 262144 | tf_op jit(solution)/shard_map/all_to_all | solution.py:191
  256.8 15.3 %all-to-all-start.24 = ((bf16[32,8,256]{2,1,0:T(8,128)(2,1)}), bf16[32,8,256]{2,1,0:T(8,128)(2,1)S(1)}, u32[]{:S(2)}, u32[]{:S(2)}) async-start(bf16[32,8,256]{2,1,0:T(8,128)(2,1)} %copy-done.113), calls=%async_computation.24 | async-start | bytes 262144 | tf_op jit(solution)/shard_map/all_to_all | solution.py:191
  272.1 13.0 %all-to-all-start.9 = ((bf16[32,8,256]{2,1,0:T(8,128)(2,1)}), bf16[32,8,256]{2,1,0:T(8,128)(2,1)S(1)}, u32[]{:S(2)}, u32[]{:S(2)}) async-start(bf16[32,8,256]{2,1,0:T(8,128)(2,1)} %copy-done.22), calls=%async_computation.9 | async-start | bytes 262144 | tf_op jit(solution)/shard_map/all_to_all | solution.py:191
  285.1 13.0 %all-to-all-start.25 = ((bf16[32,8,256]{2,1,0:T(8,128)(2,1)}), bf16[32,8,256]{2,1,0:T(8,128)(2,1)S(1)}, u32[]{:S(2)}, u32[]{:S(2)}) async-start(bf16[32,8,256]{2,1,0:T(8,128)(2,1)} %copy-done.19), calls=%async_computation.25 | async-start | bytes 262144 | tf_op jit(solution)/shard_map/all_to_all | solution.py:191
  294.9 24.6 %copy-start.15 = (bf16[256,256]{1,0:T(8,128)(2,1)S(1)}, bf16[256,256]{1,0:T(8,128)(2,1)}, u32[]{:S(2)}) copy-start(bf16[256,256]{1,0:T(8,128)(2,1)} %copy-done.14) | copy-start | bytes 393220
  298.1 15.3 %all-to-all-start.10 = ((bf16[32,8,256]{2,1,0:T(8,128)(2,1)}), bf16[32,8,256]{2,1,0:T(8,128)(2,1)S(1)}, u32[]{:S(2)}, u32[]{:S(2)}) async-start(bf16[32,8,256]{2,1,0:T(8,128)(2,1)} %copy-done.106), calls=%async_computation.10 | async-start | bytes 262144 | tf_op jit(solution)/shard_map/all_to_all | solution.py:191
  313.4 15.2 %all-to-all-start.26 = ((bf16[32,8,256]{2,1,0:T(8,128)(2,1)}), bf16[32,8,256]{2,1,0:T(8,128)(2,1)S(1)}, u32[]{:S(2)}, u32[]{:S(2)}) async-start(bf16[32,8,256]{2,1,0:T(8,128)(2,1)} %copy-done.110), calls=%async_computation.26 | async-start | bytes 262144 | tf_op jit(solution)/shard_map/all_to_all | solution.py:191
  328.6 13.0 %all-to-all-start.11 = ((bf16[32,8,256]{2,1,0:T(8,128)(2,1)}), bf16[32,8,256]{2,1,0:T(8,128)(2,1)S(1)}, u32[]{:S(2)}, u32[]{:S(2)}) async-start(bf16[32,8,256]{2,1,0:T(8,128)(2,1)} %shard_map.101), calls=%async_computation.11 | async-start | bytes 262144 | tf_op jit(solution)/shard_map/all_to_all | solution.py:191
  341.6 13.1 %all-to-all-start.27 = ((bf16[32,8,256]{2,1,0:T(8,128)(2,1)}), bf16[32,8,256]{2,1,0:T(8,128)(2,1)S(1)}, u32[]{:S(2)}, u32[]{:S(2)}) async-start(bf16[32,8,256]{2,1,0:T(8,128)(2,1)} %copy-done.20), calls=%async_computation.27 | async-start | bytes 262144 | tf_op jit(solution)/shard_map/all_to_all | solution.py:191
  351.4 24.5 %copy-start.13 = (bf16[256,256]{1,0:T(8,128)(2,1)S(1)}, bf16[256,256]{1,0:T(8,128)(2,1)}, u32[]{:S(2)}) copy-start(bf16[256,256]{1,0:T(8,128)(2,1)} %copy-done.12) | copy-start | bytes 393220
  354.7 15.2 %all-to-all-start.12 = ((bf16[32,8,256]{2,1,0:T(8,128)(2,1)}), bf16[32,8,256]{2,1,0:T(8,128)(2,1)S(1)}, u32[]{:S(2)}, u32[]{:S(2)}) async-start(bf16[32,8,256]{2,1,0:T(8,128)(2,1)} %copy-done.107), calls=%async_computation.12 | async-start | bytes 262144 | tf_op jit(solution)/shard_map/all_to_all | solution.py:191
  369.9 15.1 %all-to-all-start.28 = ((bf16[32,8,256]{2,1,0:T(8,128)(2,1)}), bf16[32,8,256]{2,1,0:T(8,128)(2,1)S(1)}, u32[]{:S(2)}, u32[]{:S(2)}) async-start(bf16[32,8,256]{2,1,0:T(8,128)(2,1)} %copy-done.111), calls=%async_computation.28 | async-start | bytes 262144 | tf_op jit(solution)/shard_map/all_to_all | solution.py:191
  385.0 13.2 %all-to-all-start.13 = ((bf16[32,8,256]{2,1,0:T(8,128)(2,1)}), bf16[32,8,256]{2,1,0:T(8,128)(2,1)S(1)}, u32[]{:S(2)}, u32[]{:S(2)}) async-start(bf16[32,8,256]{2,1,0:T(8,128)(2,1)} %shard_map.103), calls=%async_computation.13 | async-start | bytes 262144 | tf_op jit(solution)/shard_map/all_to_all | solution.py:191
  398.2 13.1 %all-to-all-start.29 = ((bf16[32,8,256]{2,1,0:T(8,128)(2,1)}), bf16[32,8,256]{2,1,0:T(8,128)(2,1)S(1)}, u32[]{:S(2)}, u32[]{:S(2)}) async-start(bf16[32,8,256]{2,1,0:T(8,128)(2,1)} %copy-done.21), calls=%async_computation.29 | async-start | bytes 262144 | tf_op jit(solution)/shard_map/all_to_all | solution.py:191
  408.0 24.5 %copy-start.11 = (bf16[256,256]{1,0:T(8,128)(2,1)S(1)}, bf16[256,256]{1,0:T(8,128)(2,1)}, u32[]{:S(2)}) copy-start(bf16[256,256]{1,0:T(8,128)(2,1)} %copy-done.10) | copy-start | bytes 393220
  411.3 15.5 %all-to-all-start.14 = ((bf16[32,8,256]{2,1,0:T(8,128)(2,1)}), bf16[32,8,256]{2,1,0:T(8,128)(2,1)S(1)}, u32[]{:S(2)}, u32[]{:S(2)}) async-start(bf16[32,8,256]{2,1,0:T(8,128)(2,1)} %copy-done.108), calls=%async_computation.14 | async-start | bytes 262144 | tf_op jit(solution)/shard_map/all_to_all | solution.py:191
  426.8 15.2 %all-to-all-start.30 = ((bf16[32,8,256]{2,1,0:T(8,128)(2,1)}), bf16[32,8,256]{2,1,0:T(8,128)(2,1)S(1)}, u32[]{:S(2)}, u32[]{:S(2)}) async-start(bf16[32,8,256]{2,1,0:T(8,128)(2,1)} %copy-done.112), calls=%async_computation.30 | async-start | bytes 262144 | tf_op jit(solution)/shard_map/all_to_all | solution.py:191
  442.0 13.7 %all-to-all-start.15 = ((bf16[32,8,256]{2,1,0:T(8,128)(2,1)}), bf16[32,8,256]{2,1,0:T(8,128)(2,1)S(1)}, u32[]{:S(2)}, u32[]{:S(2)}) async-start(bf16[32,8,256]{2,1,0:T(8,128)(2,1)} %copy-done.23), calls=%async_computation.15 | async-start | bytes 262144 | tf_op jit(solution)/shard_map/all_to_all | solution.py:191
  455.7 14.5 %all-to-all-start.31 = ((bf16[32,8,256]{2,1,0:T(8,128)(2,1)}), bf16[32,8,256]{2,1,0:T(8,128)(2,1)S(1)}, u32[]{:S(2)}, u32[]{:S(2)}) async-start(bf16[32,8,256]{2,1,0:T(8,128)(2,1)} %copy-done.18), calls=%async_computation.31 | async-start | bytes 262144 | tf_op jit(solution)/shard_map/all_to_all | solution.py:191
  464.9 2.3 copy-start.3
  465.0 2.3 copy-start.5
  465.0 2.3 copy-start.53
  465.0 2.3 copy-start.59
  465.0 2.3 copy-start.68
  465.0 2.3 copy-start.74
  467.3 1.6 copy-start.1
  467.3 1.6 copy-start.34
  467.3 1.6 copy-start.36
  471.6 37.3 %copy-start.97 = (bf16[2,512,128]{2,1,0:T(8,128)(2,1)S(1)}, bf16[2,512,128]{2,1,0:T(8,128)(2,1)}, u32[]{:S(2)}) copy-start(bf16[2,512,128]{2,1,0:T(8,128)(2,1)} %copy-done.96) | copy-start | bytes 786436
  471.6 37.3 %copy-start.99 = (bf16[2,512,128]{2,1,0:T(8,128)(2,1)S(1)}, bf16[2,512,128]{2,1,0:T(8,128)(2,1)}, u32[]{:S(2)}) copy-start(bf16[2,512,128]{2,1,0:T(8,128)(2,1)} %copy-done.98) | copy-start | bytes 786436
  472.5 47.1 %all-to-all-start.33 = ((bf16[8,320,128]{2,1,0:T(8,128)(2,1)}), bf16[8,320,128]{2,1,0:T(8,128)(2,1)S(1)}, u32[]{:S(2)}, u32[]{:S(2)}) async-start(bf16[8,320,128]{2,1,0:T(8,128)(2,1)} %bitcast.53), calls=%async_computation.33 | async-start | bytes 1310720 | tf_op jit(solution)/shard_map/all_to_all | solution.py:261
  519.6 19.4 %all-to-all-start.32 = ((bf16[8,512,128]{2,1,0:T(8,128)(2,1)}), bf16[8,512,128]{2,1,0:T(8,128)(2,1)S(1)}, u32[]{:S(2)}, u32[]{:S(2)}) async-start(bf16[8,512,128]{2,1,0:T(8,128)(2,1)} %bitcast.51), calls=%async_computation.32 | async-start | bytes 2097152 | tf_op jit(solution)/shard_map/all_to_all | solution.py:260
  (86 other events, 71.8 us)

commit v2 on v1

--- a/solution.py
+++ b/solution.py
@@ -9,7 +9,7 @@
 
 BF = jnp.bfloat16
 F32 = jnp.float32
-CHUNKS = 2
+CHUNKS = 1
 
 
 def nn(a, b):

time: 543 us -> 336 us (0.62)
  waiting for transfers between devices: 234 us -> 55.3 us
  blocking collectives: 13.6 us -> 180 us
  starting transfers between devices: 193 us -> 58.9 us
  local copies, waits for them, and re-layouts: 62.1 us -> 16.5 us
  Pallas kernels: 28.4 us -> 15.5 us
    all_to_all x32 -> x5, waiting for transfers between devices: 211 us -> 32.1 us  [swap(): return lax.all_to_all(block, ('y', 'z'), 0, 0, tiled=True)]
    all_to_all x0 -> x11, blocking collectives: none -> 167 us  [swap(): return lax.all_to_all(block, ('y', 'z'), 0, 0, tiled=True)]
    all_to_all x32 -> x5, starting transfers between devices: 149 us -> 27.3 us  [swap(): return lax.all_to_all(block, ('y', 'z'), 0, 0, tiled=True)]
    unnamed x229 -> x113, local copies, waits for them, and re-layouts: 58.8 us -> 13.2 us
    pallas_call x46 -> x27, Pallas kernels: 28.4 us -> 15.5 us  [run(): pl.pallas_call(kernel, out_shape=outs, compiler_params=pltpu.CompilerPara...]
    all_to_all x1, starting transfers between devices: 36.4 us -> 23.8 us  [shards(): w_back = lax.all_to_all(w_sent, ('x', 'c'), 0, 0, tiled=True)]
  transfers between devices with their start and end apart: 36 -> 9, of which waited for: 33 -> 7; matrix products, arithmetic and copies ran while one was open for 1% -> 2% of each run, Pallas kernels for 5% -> 2%
where the time goes in v2:
time: 336 us; the launch traced here: 334 us
  blocking collectives  180 us (54%)
  starting transfers between devices  58.9 us (18%)
  waiting for transfers between devices  55.3 us (16%)
  local copies, waits for them, and re-layouts  16.5 us (5%)
  Pallas kernels  15.5 us (5%)
  other arithmetic  6.52 us (2%)
    all_to_all x11, blocking collectives, swap(): return lax.all_to_all(block, ('y', 'z'), 0, 0, tiled=True)  167 us
    all_to_all x5, waiting for transfers between devices, swap(): return lax.all_to_all(block, ('y', 'z'), 0, 0, tiled=True)  32.1 us
    all_to_all x5, starting transfers between devices, swap(): return lax.all_to_all(block, ('y', 'z'), 0, 0, tiled=True)  27.3 us
    all_to_all x1, starting transfers between devices, shards(): w_back = lax.all_to_all(w_sent, ('x', 'c'), 0, 0, tiled=True)  23.8 us
    pallas_call x27, Pallas kernels, run(): pl.pallas_call(kernel, out_shape=outs, compiler_params=pltpu.CompilerPara...  15.5 us
    all_gather x1, blocking collectives, shards(): every = lax.all_gather(packed, ('x', 'c'), axis=0, tiled=False)  13.6 us
    all_to_all x1, waiting for transfers between devices, shards(): y_back = lax.all_to_all(y_sent, ('x', 'c'), 0, 0, tiled=True)  13.5 us
    unnamed x113, local copies, waits for them, and re-layouts  13.2 us
  transfers between devices with their start and end apart: 9, of which 7 were waited for; matrix products, arithmetic and copies ran while one was open for 2% of the time, Pallas kernels for 2%

profile of v2, /device:TPU:1, one launch (start us, length us, event | category | flops | bytes accessed | tf_op | source)
XLA Modules:
  0.0 334.2 jit_solution(3141561224193407542)
XLA Ops:
  0.6 0.9 constant_dynamic-slice_fusion
  1.6 3.3 collective-permute-start.1
  4.8 0.9 constant_dynamic-slice_fusion.1
  5.9 0.7 slice_bitcast_fusion.5
  6.6 0.9 maximum_maximum_fusion
  7.5 13.6 %all-gather = bf16[2560,128]{1,0:T(8,128)(2,1)S(1)} all-gather(bf16[320,128]{1,0:T(8,128)(2,1)S(1)} %maximum_maximum_fusion), channel_id=2, replica_groups=mesh['x'=4,'y'=4,'z'=8,'c'=2] {'x','c'}, dimensions={0}, use_global_device_ids=true | all-gather | bytes 737280 | tf_op jit(solution)/shard_map/all_gather | solution.py:177
  21.1 0.7 shard_map.86
  21.8 1.9 select_bitcast_fusion.1
  24.3 19.7 %all_to_all.90.z_ref.refs_3_ = bf16[32,8,512]{2,1,0:T(8,128)(2,1)S(1)} all-to-all(bf16[32,8,512]{2,1,0:T(8,128)(2,1)S(1)} %shard_map.87), channel_id=1, replica_groups=mesh['x'=4,'y'=4,'z'=8,'c'=2] {'y','z'}, dimensions={0} | all-to-all | bytes 524288 | tf_op jit(solution)/shard_map/all_to_all | solution.py:191
  44.0 0.9 shard_map.88
  44.9 6.6 %all-to-all-start.1 = ((bf16[32,8,512]{2,1,0:T(8,128)(2,1)}), bf16[32,8,512]{2,1,0:T(8,128)(2,1)S(1)}, u32[]{:S(2)}, u32[]{:S(2)}) async-start(bf16[32,8,512]{2,1,0:T(8,128)(2,1)} %shard_map.88), calls=%async_computation.1 | async-start | bytes 524288 | tf_op jit(solution)/shard_map/all_to_all | solution.py:191
  51.5 0.7 shard_map.89
  52.2 0.6 copy-done.34
  53.5 0.6 copy-done.46
  54.1 7.1 %all-to-all-done.1.u_ref = bf16[32,8,512]{2,1,0:T(8,128)(2,1)S(1)} async-done(((bf16[32,8,512]{2,1,0:T(8,128)(2,1)}), bf16[32,8,512]{2,1,0:T(8,128)(2,1)S(1)}, u32[]{:S(2)}, u32[]{:S(2)}) %all-to-all-start.1) | async-done | bytes 262176 | tf_op jit(solution)/shard_map/all_to_all | solution.py:191
  61.7 15.6 %all_to_all.91.z_ref.refs_3_ = bf16[32,8,512]{2,1,0:T(8,128)(2,1)S(1)} all-to-all(bf16[32,8,512]{2,1,0:T(8,128)(2,1)S(1)} %get-tuple-element.58), channel_id=1, replica_groups=mesh['x'=4,'y'=4,'z'=8,'c'=2] {'y','z'}, dimensions={0} | all-to-all | bytes 524288 | tf_op jit(solution)/shard_map/all_to_all | solution.py:191
  77.3 0.9 shard_map.91
  78.2 5.5 %all-to-all-start.3 = ((bf16[32,8,512]{2,1,0:T(8,128)(2,1)}), bf16[32,8,512]{2,1,0:T(8,128)(2,1)S(1)}, u32[]{:S(2)}, u32[]{:S(2)}) async-start(bf16[32,8,512]{2,1,0:T(8,128)(2,1)} %shard_map.91), calls=%async_computation.3 | async-start | bytes 524288 | tf_op jit(solution)/shard_map/all_to_all | solution.py:191
  83.7 0.7 shard_map.92
  84.4 0.7 copy-done.36
  85.1 0.6 copy-done.50
  85.7 7.7 %all-to-all-done.3.u_ref = bf16[32,8,512]{2,1,0:T(8,128)(2,1)S(1)} async-done(((bf16[32,8,512]{2,1,0:T(8,128)(2,1)}), bf16[32,8,512]{2,1,0:T(8,128)(2,1)S(1)}, u32[]{:S(2)}, u32[]{:S(2)}) %all-to-all-start.3) | async-done | bytes 262176 | tf_op jit(solution)/shard_map/all_to_all | solution.py:191
  93.9 14.2 %all_to_all.92.z_ref.refs_3_ = bf16[32,8,512]{2,1,0:T(8,128)(2,1)S(1)} all-to-all(bf16[32,8,512]{2,1,0:T(8,128)(2,1)S(1)} %get-tuple-element.63), channel_id=1, replica_groups=mesh['x'=4,'y'=4,'z'=8,'c'=2] {'y','z'}, dimensions={0} | all-to-all | bytes 524288 | tf_op jit(solution)/shard_map/all_to_all | solution.py:191
  108.0 0.9 shard_map.94
  109.0 4.6 %all-to-all-start.5 = ((bf16[32,8,512]{2,1,0:T(8,128)(2,1)}), bf16[32,8,512]{2,1,0:T(8,128)(2,1)S(1)}, u32[]{:S(2)}, u32[]{:S(2)}) async-start(bf16[32,8,512]{2,1,0:T(8,128)(2,1)} %shard_map.94), calls=%async_computation.5 | async-start | bytes 524288 | tf_op jit(solution)/shard_map/all_to_all | solution.py:191
  113.5 0.7 shard_map.95
  114.9 0.7 copy-done.40
  115.5 0.6 copy-done.42
  116.2 0.7 copy-done.54
  116.8 6.4 %all-to-all-done.5.u_ref = bf16[32,8,512]{2,1,0:T(8,128)(2,1)S(1)} async-done(((bf16[32,8,512]{2,1,0:T(8,128)(2,1)}), bf16[32,8,512]{2,1,0:T(8,128)(2,1)S(1)}, u32[]{:S(2)}, u32[]{:S(2)}) %all-to-all-start.5) | async-done | bytes 262176 | tf_op jit(solution)/shard_map/all_to_all | solution.py:191
  123.7 13.9 %all_to_all.93.z_ref.refs_3_ = bf16[32,8,512]{2,1,0:T(8,128)(2,1)S(1)} all-to-all(bf16[32,8,512]{2,1,0:T(8,128)(2,1)S(1)} %get-tuple-element.68), channel_id=1, replica_groups=mesh['x'=4,'y'=4,'z'=8,'c'=2] {'y','z'}, dimensions={0} | all-to-all | bytes 524288 | tf_op jit(solution)/shard_map/all_to_all | solution.py:191
  137.6 0.9 shard_map.97
  138.5 4.4 %all-to-all-start.7 = ((bf16[32,8,512]{2,1,0:T(8,128)(2,1)}), bf16[32,8,512]{2,1,0:T(8,128)(2,1)S(1)}, u32[]{:S(2)}, u32[]{:S(2)}) async-start(bf16[32,8,512]{2,1,0:T(8,128)(2,1)} %shard_map.97), calls=%async_computation.7 | async-start | bytes 524288 | tf_op jit(solution)/shard_map/all_to_all | solution.py:191
  142.9 1.0 pad_maximum_fusion.3.x_ref
  144.2 8.3 %all-to-all-done.7.u_ref = bf16[32,8,512]{2,1,0:T(8,128)(2,1)S(1)} async-done(((bf16[32,8,512]{2,1,0:T(8,128)(2,1)}), bf16[32,8,512]{2,1,0:T(8,128)(2,1)S(1)}, u32[]{:S(2)}, u32[]{:S(2)}) %all-to-all-start.7) | async-done | bytes 262176 | tf_op jit(solution)/shard_map/all_to_all | solution.py:191
  152.6 0.9 copy-done.41
  153.9 14.0 %all_to_all.94.z_ref.refs_4_ = bf16[32,8,512]{2,1,0:T(8,128)(2,1)S(1)} all-to-all(bf16[32,8,512]{2,1,0:T(8,128)(2,1)S(1)} %get-tuple-element.71), channel_id=1, replica_groups=mesh['x'=4,'y'=4,'z'=8,'c'=2] {'y','z'}, dimensions={0} | all-to-all | bytes 524288 | tf_op jit(solution)/shard_map/all_to_all | solution.py:191
  168.1 13.9 %all_to_all.95.gz_ref.refs_1_ = bf16[32,8,512]{2,1,0:T(8,128)(2,1)S(1)} all-to-all(bf16[32,8,512]{2,1,0:T(8,128)(2,1)S(1)} %shard_map.99), channel_id=1, replica_groups=mesh['x'=4,'y'=4,'z'=8,'c'=2] {'y','z'}, dimensions={0} | all-to-all | bytes 524288 | tf_op jit(solution)/shard_map/all_to_all | solution.py:191
  182.6 14.2 %all_to_all.96.z_ref.refs_4_ = bf16[32,8,512]{2,1,0:T(8,128)(2,1)S(1)} all-to-all(bf16[32,8,512]{2,1,0:T(8,128)(2,1)S(1)} %get-tuple-element.77), channel_id=1, replica_groups=mesh['x'=4,'y'=4,'z'=8,'c'=2] {'y','z'}, dimensions={0} | all-to-all | bytes 524288 | tf_op jit(solution)/shard_map/all_to_all | solution.py:191
  197.0 15.2 %all_to_all.97.gz_ref.refs_1_ = bf16[32,8,512]{2,1,0:T(8,128)(2,1)S(1)} all-to-all(bf16[32,8,512]{2,1,0:T(8,128)(2,1)S(1)} %shard_map.101), channel_id=1, replica_groups=mesh['x'=4,'y'=4,'z'=8,'c'=2] {'y','z'}, dimensions={0} | all-to-all | bytes 524288 | tf_op jit(solution)/shard_map/all_to_all | solution.py:191
  212.9 15.6 %all_to_all.98.z_ref.refs_4_ = bf16[32,8,512]{2,1,0:T(8,128)(2,1)S(1)} all-to-all(bf16[32,8,512]{2,1,0:T(8,128)(2,1)S(1)} %get-tuple-element.83), channel_id=1, replica_groups=mesh['x'=4,'y'=4,'z'=8,'c'=2] {'y','z'}, dimensions={0} | all-to-all | bytes 524288 | tf_op jit(solution)/shard_map/all_to_all | solution.py:191
  228.7 14.5 %all_to_all.99.gz_ref.refs_1_ = bf16[32,8,512]{2,1,0:T(8,128)(2,1)S(1)} all-to-all(bf16[32,8,512]{2,1,0:T(8,128)(2,1)S(1)} %shard_map.103), channel_id=1, replica_groups=mesh['x'=4,'y'=4,'z'=8,'c'=2] {'y','z'}, dimensions={0} | all-to-all | bytes 524288 | tf_op jit(solution)/shard_map/all_to_all | solution.py:191
  243.7 0.7 copy-done.12
  244.4 15.7 %all_to_all.100.z_ref.refs_4_ = bf16[32,8,512]{2,1,0:T(8,128)(2,1)S(1)} all-to-all(bf16[32,8,512]{2,1,0:T(8,128)(2,1)S(1)} %get-tuple-element.88), channel_id=1, replica_groups=mesh['x'=4,'y'=4,'z'=8,'c'=2] {'y','z'}, dimensions={0} | all-to-all | bytes 524288 | tf_op jit(solution)/shard_map/all_to_all | solution.py:191
  260.1 0.9 shard_map.105
  261.1 6.4 %all-to-all-start.15 = ((bf16[32,8,512]{2,1,0:T(8,128)(2,1)}), bf16[32,8,512]{2,1,0:T(8,128)(2,1)S(1)}, u32[]{:S(2)}, u32[]{:S(2)}) async-start(bf16[32,8,512]{2,1,0:T(8,128)(2,1)} %shard_map.105), calls=%async_computation.15 | async-start | bytes 524288 | tf_op jit(solution)/shard_map/all_to_all | solution.py:191
  267.4 0.9 copy-done.9
  268.4 0.9 copy-done.15
  269.3 0.9 copy-done.19
  270.3 0.8 shard_map.110
  271.1 0.7 copy-done.24
  271.8 0.7 copy-done.26
  272.5 0.8 shard_map.109
  273.6 0.8 shard_map.108
  274.4 2.7 all-to-all-done.15.gz_ref.refs_1_
  277.4 0.8 shard_map.107
  278.3 0.9 pad_maximum_fusion.1
  279.3 23.8 %all-to-all-start.17 = ((bf16[8,320,128]{2,1,0:T(8,128)(2,1)}), bf16[8,320,128]{2,1,0:T(8,128)(2,1)S(1)}, u32[]{:S(2)}, u32[]{:S(2)}) async-start(bf16[8,320,128]{2,1,0:T(8,128)(2,1)} %bitcast.22), calls=%async_computation.17 | async-start | bytes 1310720 | tf_op jit(solution)/shard_map/all_to_all | solution.py:261
  303.0 1.1 pad_maximum_fusion
  304.2 9.6 %all-to-all-done.17 = bf16[8,320,128]{2,1,0:T(8,128)(2,1)S(1)} async-done(((bf16[8,320,128]{2,1,0:T(8,128)(2,1)}), bf16[8,320,128]{2,1,0:T(8,128)(2,1)S(1)}, u32[]{:S(2)}, u32[]{:S(2)}) %all-to-all-start.17) | async-done | bytes 655392 | tf_op jit(solution)/shard_map/all_to_all | solution.py:261
  313.8 4.4 %all-to-all-start.16 = ((bf16[8,512,128]{2,1,0:T(8,128)(2,1)}), bf16[8,512,128]{2,1,0:T(8,128)(2,1)S(1)}, u32[]{:S(2)}, u32[]{:S(2)}) async-start(bf16[8,512,128]{2,1,0:T(8,128)(2,1)} %bitcast.16), calls=%async_computation.16 | async-start | bytes 2097152 | tf_op jit(solution)/shard_map/all_to_all | solution.py:260
  319.0 0.7 slice_bitcast_fusion
  319.7 13.5 %all-to-all-done.16 = bf16[8,512,128]{2,1,0:T(8,128)(2,1)S(1)} async-done(((bf16[8,512,128]{2,1,0:T(8,128)(2,1)}), bf16[8,512,128]{2,1,0:T(8,128)(2,1)S(1)}, u32[]{:S(2)}, u32[]{:S(2)}) %all-to-all-start.16) | async-done | bytes 1048608 | tf_op jit(solution)/shard_map/all_to_all | solution.py:260
  333.2 1.0 copy.10
  (120 shorter events, 7.9 us)
Async XLA Ops:
  1.6 20.2 %collective-permute-start.1 = (bf16[512,128]{1,0:T(8,128)(2,1)S(1)}, bf16[512,128]{1,0:T(8,128)(2,1)S(1)}, u32[]{:S(2)}, u32[]{:S(2)}) collective-permute-start(bf16[512,128]{1,0:T(8,128)(2,1)S(1)} %constant_dynamic-slice_fusion), channel_id=1, source_target_pairs={{0,1},{1,0},{2,3},{3,2},{4,5},{5,4},{6,7},{7,6},{8,9},{9,8},{10,11... | collective-permute-start | bytes 393224 | tf_op jit(solution)/shard_map/ppermute | solution.py:184
  5.8 16.0 %collective-permute-start = (bf16[512,128]{1,0:T(8,128)(2,1)S(1)}, bf16[512,128]{1,0:T(8,128)(2,1)S(1)}, u32[]{:S(2)}, u32[]{:S(2)}) collective-permute-start(bf16[512,128]{1,0:T(8,128)(2,1)S(1)} %constant_dynamic-slice_fusion.1), channel_id=1, source_target_pairs={{0,1},{1,0},{2,3},{3,2},{4,5},{5,4},{6,7},{7,6},{8,9},{9,8},{10,11... | collective-permute-start | bytes 393224 | tf_op jit(solution)/shard_map/ppermute | solution.py:184
  21.7 1.9 copy-start.28
  21.8 2.3 copy-start.30
  21.8 2.3 copy-start.32
  44.9 16.2 %all-to-all-start.1 = ((bf16[32,8,512]{2,1,0:T(8,128)(2,1)}), bf16[32,8,512]{2,1,0:T(8,128)(2,1)S(1)}, u32[]{:S(2)}, u32[]{:S(2)}) async-start(bf16[32,8,512]{2,1,0:T(8,128)(2,1)} %shard_map.88), calls=%async_computation.1 | async-start | bytes 524288 | tf_op jit(solution)/shard_map/all_to_all | solution.py:191
  52.2 0.7 copy-start.34
  52.8 0.6 copy-start.44
  53.5 0.7 copy-start.46
  54.1 39.2 %copy-start.4 = (bf16[256,256]{1,0:T(8,128)(2,1)}, bf16[256,256]{1,0:T(8,128)(2,1)S(1)}, u32[]{:S(2)}) copy-start(bf16[256,256]{1,0:T(8,128)(2,1)S(1)} %get-tuple-element.60.gt_ref) | copy-start | bytes 393220
  78.2 15.1 %all-to-all-start.3 = ((bf16[32,8,512]{2,1,0:T(8,128)(2,1)}), bf16[32,8,512]{2,1,0:T(8,128)(2,1)S(1)}, u32[]{:S(2)}, u32[]{:S(2)}) async-start(bf16[32,8,512]{2,1,0:T(8,128)(2,1)} %shard_map.91), calls=%async_computation.3 | async-start | bytes 524288 | tf_op jit(solution)/shard_map/all_to_all | solution.py:191
  84.4 0.7 copy-start.36
  85.0 0.6 copy-start.50
  85.7 8.2 %copy-start.48 = (bf16[256,256]{1,0:T(8,128)(2,1)}, bf16[256,256]{1,0:T(8,128)(2,1)S(1)}, u32[]{:S(2)}) copy-start(bf16[256,256]{1,0:T(8,128)(2,1)S(1)} %get-tuple-element.80.r_ref) | copy-start | bytes 393220
  85.7 37.5 %copy-start.6 = (bf16[256,256]{1,0:T(8,128)(2,1)}, bf16[256,256]{1,0:T(8,128)(2,1)S(1)}, u32[]{:S(2)}) copy-start(bf16[256,256]{1,0:T(8,128)(2,1)S(1)} %get-tuple-element.65.gt_ref) | copy-start | bytes 393220
  109.0 14.2 %all-to-all-start.5 = ((bf16[32,8,512]{2,1,0:T(8,128)(2,1)}), bf16[32,8,512]{2,1,0:T(8,128)(2,1)S(1)}, u32[]{:S(2)}, u32[]{:S(2)}) async-start(bf16[32,8,512]{2,1,0:T(8,128)(2,1)} %shard_map.94), calls=%async_computation.5 | async-start | bytes 524288 | tf_op jit(solution)/shard_map/all_to_all | solution.py:191
  114.9 0.7 copy-start.40
  115.5 0.6 copy-start.42
  116.2 0.7 copy-start.54
  116.8 6.9 %copy-start.52 = (bf16[256,256]{1,0:T(8,128)(2,1)}, bf16[256,256]{1,0:T(8,128)(2,1)S(1)}, u32[]{:S(2)}) copy-start(bf16[256,256]{1,0:T(8,128)(2,1)S(1)} %get-tuple-element.74.r_ref) | copy-start | bytes 393220
  123.2 14.4 %copy-start.43 = (bf16[256,256]{1,0:T(8,128)(2,1)S(1)}, bf16[256,256]{1,0:T(8,128)(2,1)}, u32[]{:S(2)}) copy-start(bf16[256,256]{1,0:T(8,128)(2,1)} %copy-done.42) | copy-start | bytes 393220
  123.7 28.9 %copy-start.8 = (bf16[256,512]{1,0:T(8,128)(2,1)}, bf16[256,512]{1,0:T(8,128)(2,1)S(1)}, u32[]{:S(2)}) copy-start(bf16[256,512]{1,0:T(8,128)(2,1)S(1)} %get-tuple-element.67.x_ref.refs_0_) | copy-start | bytes 786436
  138.5 14.0 %all-to-all-start.7 = ((bf16[32,8,512]{2,1,0:T(8,128)(2,1)}), bf16[32,8,512]{2,1,0:T(8,128)(2,1)S(1)}, u32[]{:S(2)}, u32[]{:S(2)}) async-start(bf16[32,8,512]{2,1,0:T(8,128)(2,1)} %shard_map.97), calls=%async_computation.7 | async-start | bytes 524288 | tf_op jit(solution)/shard_map/all_to_all | solution.py:191
  152.6 15.3 %copy-start.39 = (bf16[256,256]{1,0:T(8,128)(2,1)S(1)}, bf16[256,256]{1,0:T(8,128)(2,1)}, u32[]{:S(2)}) copy-start(bf16[256,256]{1,0:T(8,128)(2,1)} %copy-done.38) | copy-start | bytes 393220
  152.6 0.9 copy-start.41
  153.9 28.1 %copy-start.14 = (bf16[256,512]{1,0:T(8,128)(2,1)}, bf16[256,512]{1,0:T(8,128)(2,1)S(1)}, u32[]{:S(2)}) copy-start(bf16[256,512]{1,0:T(8,128)(2,1)S(1)} %get-tuple-element.73.gg_ref.refs_2_) | copy-start | bytes 786436
  153.9 28.1 %copy-start.7 = (bf16[256,256]{1,0:T(8,128)(2,1)S(1)}, bf16[256,256]{1,0:T(8,128)(2,1)}, u32[]{:S(2)}) copy-start(bf16[256,256]{1,0:T(8,128)(2,1)} %copy-done.6) | copy-start | bytes 393220
  153.9 28.1 %copy-start.53 = (bf16[256,256]{1,0:T(8,128)(2,1)S(1)}, bf16[256,256]{1,0:T(8,128)(2,1)}, u32[]{:S(2)}) copy-start(bf16[256,256]{1,0:T(8,128)(2,1)} %copy-done.52) | copy-start | bytes 393220
  153.9 28.1 %copy-start.55 = (bf16[256,256]{1,0:T(8,128)(2,1)S(1)}, bf16[256,256]{1,0:T(8,128)(2,1)}, u32[]{:S(2)}) copy-start(bf16[256,256]{1,0:T(8,128)(2,1)} %copy-done.54) | copy-start | bytes 393220
  182.0 14.8 %copy-start.37 = (bf16[256,256]{1,0:T(8,128)(2,1)S(1)}, bf16[256,256]{1,0:T(8,128)(2,1)}, u32[]{:S(2)}) copy-start(bf16[256,256]{1,0:T(8,128)(2,1)} %copy-done.36) | copy-start | bytes 393220
  182.5 30.3 %copy-start.16 = (bf16[256,512]{1,0:T(8,128)(2,1)}, bf16[256,512]{1,0:T(8,128)(2,1)S(1)}, u32[]{:S(2)}) copy-start(bf16[256,512]{1,0:T(8,128)(2,1)S(1)} %get-tuple-element.79.gg_ref.refs_2_) | copy-start | bytes 786436
  182.5 30.3 %copy-start.18 = (bf16[256,512]{1,0:T(8,128)(2,1)}, bf16[256,512]{1,0:T(8,128)(2,1)S(1)}, u32[]{:S(2)}) copy-start(bf16[256,512]{1,0:T(8,128)(2,1)S(1)} %get-tuple-element.76.y_ref.refs_5_) | copy-start | bytes 786436
  182.6 29.7 %copy-start.5 = (bf16[256,256]{1,0:T(8,128)(2,1)S(1)}, bf16[256,256]{1,0:T(8,128)(2,1)}, u32[]{:S(2)}) copy-start(bf16[256,256]{1,0:T(8,128)(2,1)} %copy-done.4) | copy-start | bytes 393220
  182.6 29.7 %copy-start.49 = (bf16[256,256]{1,0:T(8,128)(2,1)S(1)}, bf16[256,256]{1,0:T(8,128)(2,1)}, u32[]{:S(2)}) copy-start(bf16[256,256]{1,0:T(8,128)(2,1)} %copy-done.48) | copy-start | bytes 393220
  182.6 29.7 %copy-start.51 = (bf16[256,256]{1,0:T(8,128)(2,1)S(1)}, bf16[256,256]{1,0:T(8,128)(2,1)}, u32[]{:S(2)}) copy-start(bf16[256,256]{1,0:T(8,128)(2,1)} %copy-done.50) | copy-start | bytes 393220
  212.3 16.1 %copy-start = (bf16[32,8,512]{2,1,0:T(8,128)(2,1)}, bf16[32,8,512]{2,1,0:T(8,128)(2,1)S(1)}, u32[]{:S(2)}) copy-start(bf16[32,8,512]{2,1,0:T(8,128)(2,1)S(1)} %all_to_all.97.gz_ref.refs_1_) | copy-start | bytes 786436
  212.3 16.1 %copy-start.35 = (bf16[256,256]{1,0:T(8,128)(2,1)S(1)}, bf16[256,256]{1,0:T(8,128)(2,1)}, u32[]{:S(2)}) copy-start(bf16[256,256]{1,0:T(8,128)(2,1)} %copy-done.34) | copy-start | bytes 393220
  212.8 30.9 %copy-start.20 = (bf16[256,512]{1,0:T(8,128)(2,1)}, bf16[256,512]{1,0:T(8,128)(2,1)S(1)}, u32[]{:S(2)}) copy-start(bf16[256,512]{1,0:T(8,128)(2,1)S(1)} %get-tuple-element.85.gg_ref.refs_2_) | copy-start | bytes 786436
  212.8 30.9 %copy-start.22 = (bf16[256,512]{1,0:T(8,128)(2,1)}, bf16[256,512]{1,0:T(8,128)(2,1)S(1)}, u32[]{:S(2)}) copy-start(bf16[256,512]{1,0:T(8,128)(2,1)S(1)} %get-tuple-element.82.y_ref.refs_5_) | copy-start | bytes 786436
  212.8 30.4 %copy-start.45 = (bf16[256,256]{1,0:T(8,128)(2,1)S(1)}, bf16[256,256]{1,0:T(8,128)(2,1)}, u32[]{:S(2)}) copy-start(bf16[256,256]{1,0:T(8,128)(2,1)} %copy-done.44) | copy-start | bytes 393220
  212.8 30.4 %copy-start.47 = (bf16[256,256]{1,0:T(8,128)(2,1)S(1)}, bf16[256,256]{1,0:T(8,128)(2,1)}, u32[]{:S(2)}) copy-start(bf16[256,256]{1,0:T(8,128)(2,1)} %copy-done.46) | copy-start | bytes 393220
  243.2 16.9 %copy-start.2 = (bf16[32,8,512]{2,1,0:T(8,128)(2,1)}, bf16[32,8,512]{2,1,0:T(8,128)(2,1)S(1)}, u32[]{:S(2)}) copy-start(bf16[32,8,512]{2,1,0:T(8,128)(2,1)S(1)} %all_to_all.99.gz_ref.refs_1_) | copy-start | bytes 786436
  243.2 16.9 %copy-start.33 = (bf16[256,256]{1,0:T(8,128)(2,1)S(1)}, bf16[256,256]{1,0:T(8,128)(2,1)}, u32[]{:S(2)}) copy-start(bf16[256,256]{1,0:T(8,128)(2,1)} %copy-done.32) | copy-start | bytes 393220
  243.7 0.7 copy-start.12
  244.4 15.7 %copy-start.10 = (bf16[256,512]{1,0:T(8,128)(2,1)}, bf16[256,512]{1,0:T(8,128)(2,1)S(1)}, u32[]{:S(2)}) copy-start(bf16[256,512]{1,0:T(8,128)(2,1)S(1)} %get-tuple-element.90.gg_ref.refs_2_) | copy-start | bytes 786436
  261.1 16.0 %all-to-all-start.15 = ((bf16[32,8,512]{2,1,0:T(8,128)(2,1)}), bf16[32,8,512]{2,1,0:T(8,128)(2,1)S(1)}, u32[]{:S(2)}, u32[]{:S(2)}) async-start(bf16[32,8,512]{2,1,0:T(8,128)(2,1)} %shard_map.105), calls=%async_computation.15 | async-start | bytes 524288 | tf_op jit(solution)/shard_map/all_to_all | solution.py:191
  267.4 1.0 copy-start.9
  268.4 0.9 copy-start.15
  269.3 0.9 copy-start.19
  270.3 2.2 copy-start.1
  270.3 2.2 copy-start.17
  270.3 2.2 copy-start.23
  271.1 0.7 copy-start.24
  271.8 0.7 copy-start.26
  272.5 1.0 copy-start.3
  272.5 1.0 copy-start.13
  272.5 1.1 copy-start.21
  273.6 3.5 %copy-start.11 = (bf16[256,512]{1,0:T(8,128)(2,1)S(1)}, bf16[256,512]{1,0:T(8,128)(2,1)}, u32[]{:S(2)}) copy-start(bf16[256,512]{1,0:T(8,128)(2,1)} %copy-done.10) | copy-start | bytes 786436
  273.6 3.5 %copy-start.29 = (bf16[256,256]{1,0:T(8,128)(2,1)S(1)}, bf16[256,256]{1,0:T(8,128)(2,1)}, u32[]{:S(2)}) copy-start(bf16[256,256]{1,0:T(8,128)(2,1)} %copy-done.28) | copy-start | bytes 393220
  273.6 3.5 %copy-start.31 = (bf16[256,256]{1,0:T(8,128)(2,1)S(1)}, bf16[256,256]{1,0:T(8,128)(2,1)}, u32[]{:S(2)}) copy-start(bf16[256,256]{1,0:T(8,128)(2,1)} %copy-done.30) | copy-start | bytes 393220
  277.4 0.9 copy-start.27
  278.3 24.7 %copy-start.25 = (bf16[2,512,128]{2,1,0:T(8,128)(2,1)S(1)}, bf16[2,512,128]{2,1,0:T(8,128)(2,1)}, u32[]{:S(2)}) copy-start(bf16[2,512,128]{2,1,0:T(8,128)(2,1)} %copy-done.24) | copy-start | bytes 786436
  279.3 34.5 %all-to-all-start.17 = ((bf16[8,320,128]{2,1,0:T(8,128)(2,1)}), bf16[8,320,128]{2,1,0:T(8,128)(2,1)S(1)}, u32[]{:S(2)}, u32[]{:S(2)}) async-start(bf16[8,320,128]{2,1,0:T(8,128)(2,1)} %bitcast.22), calls=%async_computation.17 | async-start | bytes 1310720 | tf_op jit(solution)/shard_map/all_to_all | solution.py:261
  313.8 19.4 %all-to-all-start.16 = ((bf16[8,512,128]{2,1,0:T(8,128)(2,1)}), bf16[8,512,128]{2,1,0:T(8,128)(2,1)S(1)}, u32[]{:S(2)}, u32[]{:S(2)}) async-start(bf16[8,512,128]{2,1,0:T(8,128)(2,1)} %bitcast.16), calls=%async_computation.16 | async-start | bytes 2097152 | tf_op jit(solution)/shard_map/all_to_all | solution.py:260
  (1 other events, 0.6 us)
